TPU v7x, 512 devices: a whole 4x4x16 slice. The times are simulated.
512 devices in a mesh: region: 64 (over x, z), rays: 8 (over y, core).
Axes of the slice: x: 4, y: 4, z: 16, core: 2. Of those that a mesh axis runs over, the one named last changes fastest.
Arguments:
- ray_codes: bfloat16 [2, 4096, 128], P(None, 'rays'), may hold values from -6 to 6
- target: bfloat16 [4096, 384], P('rays'), may hold values from -0.19921875 to 1
- direction: int32 [4096], P('rays'), may hold values from 0 to 1
- entries: int32 [64, 4096], P('region', 'rays'), may hold values from 0 to 4
- exits: int32 [64, 4096], P('region', 'rays'), may hold values from 4 to 8
- depth_bins: int32 [64, 8, 4096], P('region', None, 'rays'), may hold values from 0 to 63, as said below
- in_layer: float32 [3, 64, 128, 256], P(None, 'region', 'rays'), as said below
- mid_layer: float32 [3, 64, 256, 256], P(None, 'region', 'rays'), as said below
- feat_layer: float32 [3, 64, 256, 384], P(None, 'region', 'rays'), as said below
- vectors: float32 [3, 64, 1152], P(None, 'region', 'rays'), as said below
Outputs:
- new_in_layer: float32 [3, 64, 128, 256], P(None, 'region', 'rays')
- new_mid_layer: float32 [3, 64, 256, 256], P(None, 'region', 'rays')
- new_feat_layer: float32 [3, 64, 256, 384], P(None, 'region', 'rays')
- new_vectors: float32 [3, 64, 1152], P(None, 'region', 'rays')
- depth_grad: float32 [64, 4096], P('region', 'rays')
Inputs may be any that keep to these rules, and one draw needn't show every extreme that they name: `direction`: 0: the ray meets the regions in increasing index order; 1: in decreasing order. A ray's samples inside a region are the slots j with entries <= j < exits. `depth_bins`: slot j lies in bins j * (8) to (j + 1) * 8 - 1. `in_layer`: the second moments (index 2 of the first dimension) are positive. `mid_layer`: the second moments (index 2 of the first dimension) are positive. `feat_layer`: the second moments (index 2 of the first dimension) are positive. `vectors`: the second moments (index 2 of the first dimension) are positive.
All inputs are finite; a program needn't handle non-finite values.
Results may differ from a plain program's by a relative error of at most 0.0025.
The roundings to bfloat16 on the way count: a program that leaves them out, or rounds other values in their place, can miss the bound.
Values may be sent and summed in bfloat16 or wider, within the bound.
A program may use at most 64 MiB of HBM per device.

v0:
```python
import jax
import jax.numpy as jnp
from jax import lax
from jax.sharding import PartitionSpec as P

BINS = 64


depth_scale = 4.0
beta_one = 0.9
beta_two = 0.999
learn_rate = 0.001
epsilon = 1e-08
first_fix = 1.0 - 0.9**10
second_fix = 1.0 - 0.999**10


def entering(value, axis, join, neutral, backward):
    count, mine = (lax.axis_size(axis), lax.axis_index(axis))
    pieces = lax.all_gather(value, axis)
    if backward:
        pieces = pieces[::-1]
        mine = count - 1 - mine
    total = jnp.full_like(value, 0) + jnp.asarray(neutral, value.dtype)

    def lap(position, total):
        longer = join(total, pieces[position])
        return jnp.where(position < mine, longer, total)

    return lax.fori_loop(0, count - 1, lap, total)


def forward(ray_codes, depth_bins, entry_row, exit_row, weights, unit_length):
    in_weight, mid_weight, feat_weight, vec_weight = weights
    hidden_width = in_weight.shape[1]
    bias_one = vec_weight[:hidden_width].astype(jnp.float32)
    bias_two = vec_weight[hidden_width : 2 * hidden_width].astype(jnp.float32)
    density_weight = vec_weight[2 * hidden_width : 3 * hidden_width]
    bias_feat = vec_weight[3 * hidden_width :].astype(jnp.float32)
    samples, ray_count = depth_bins.shape
    bin_float = depth_bins.astype(jnp.float32)
    following = jnp.concatenate(
        [bin_float[1:], jnp.full((1, ray_count), float(BINS), jnp.float32)], 0
    )
    spacing = (following - bin_float) * unit_length
    position = (bin_float + 0.5) / BINS
    sample_slot = lax.broadcasted_iota(jnp.int32, (samples, ray_count), 0)
    inside = ((sample_slot >= entry_row[None, :]) & (sample_slot < exit_row[None, :])).astype(
        jnp.float32
    )
    codes_float = ray_codes.astype(jnp.float32)
    encoded = (codes_float[0][None] + position[:, :, None] * codes_float[1][None]).astype(
        jnp.bfloat16
    )
    encoded = encoded.reshape(samples * ray_count, codes_float.shape[2])
    hidden_one = jnp.maximum(
        jnp.dot(encoded, in_weight, preferred_element_type=jnp.float32) + bias_one, 0.0
    ).astype(jnp.bfloat16)
    hidden_two = jnp.maximum(
        jnp.dot(hidden_one, mid_weight, preferred_element_type=jnp.float32) + bias_two, 0.0
    ).astype(jnp.bfloat16)
    density_raw = jnp.dot(hidden_two, density_weight, preferred_element_type=jnp.float32).reshape(
        samples, ray_count
    )
    colour = jax.nn.sigmoid(
        jnp.dot(hidden_two, feat_weight, preferred_element_type=jnp.float32) + bias_feat
    )
    colour = colour.reshape(samples, ray_count, feat_weight.shape[1])
    optical = jax.nn.softplus(density_raw) * spacing * inside
    optical_before = jnp.cumsum(optical, 0) - optical
    local_weight = jnp.exp(-optical_before) * -jnp.expm1(-optical)
    return (
        encoded,
        hidden_one,
        hidden_two,
        density_raw,
        colour,
        optical,
        optical_before,
        local_weight,
        spacing,
        inside,
    )


def backward(found, weights, entry_trans, after_sum, feature_grad):
    (
        encoded,
        hidden_one,
        hidden_two,
        density_raw,
        colour,
        optical,
        optical_before,
        local_weight,
        spacing,
        inside,
    ) = found
    in_weight, mid_weight, feat_weight, vec_weight = weights
    hidden_width = in_weight.shape[1]
    density_weight = vec_weight[2 * hidden_width : 3 * hidden_width]
    grad_float = feature_grad.astype(jnp.float32)
    sample_grad = jnp.sum(colour * grad_float[None], -1)
    weighted = local_weight * sample_grad
    later_local = jnp.cumsum(weighted[::-1], 0)[::-1] - weighted
    optical_grad = (
        entry_trans[None] * (jnp.exp(-(optical_before + optical)) * sample_grad - later_local)
        - after_sum[None]
    )
    density_grad = (
        (optical_grad * spacing * inside * jax.nn.sigmoid(density_raw))
        .astype(jnp.bfloat16)
        .reshape(-1)
    )
    colour_grad = (
        (entry_trans[None] * local_weight)[:, :, None] * grad_float[None] * colour * (1.0 - colour)
    ).astype(jnp.bfloat16)
    colour_grad = colour_grad.reshape(-1, colour.shape[2])
    hidden_grad = jnp.dot(colour_grad, feat_weight.T, preferred_element_type=jnp.float32)
    hidden_grad = (
        hidden_grad
        + density_grad.astype(jnp.float32)[:, None] * density_weight.astype(jnp.float32)[None, :]
    )
    second_grad = (hidden_grad * (hidden_two > 0)).astype(jnp.bfloat16)
    first_grad = (
        jnp.dot(second_grad, mid_weight.T, preferred_element_type=jnp.float32) * (hidden_one > 0)
    ).astype(jnp.bfloat16)
    in_grad = jnp.dot(encoded.T, first_grad, preferred_element_type=jnp.float32)
    mid_grad = jnp.dot(hidden_one.T, second_grad, preferred_element_type=jnp.float32)
    feat_grad = jnp.dot(hidden_two.T, colour_grad, preferred_element_type=jnp.float32)
    density_sum = jnp.dot(density_grad, hidden_two, preferred_element_type=jnp.float32)
    vec_grad = jnp.concatenate(
        [
            jnp.sum(first_grad, 0, dtype=jnp.float32),
            jnp.sum(second_grad, 0, dtype=jnp.float32),
            density_sum,
            jnp.sum(colour_grad, 0, dtype=jnp.float32),
        ]
    )
    return (in_grad, mid_grad, feat_grad, vec_grad)


def adam_update(stacked, gradient):
    first_moment = beta_one * stacked[1] + (1.0 - beta_one) * gradient
    second = beta_two * stacked[2] + (1.0 - beta_two) * gradient * gradient
    update_step = first_moment / first_fix / (jnp.sqrt(second / second_fix) + epsilon)
    return jnp.stack([stacked[0] - learn_rate * update_step, first_moment, second])


def per_device(
    ray_codes,
    target,
    direction,
    entries,
    exits,
    depth_bins,
    in_layer,
    mid_layer,
    feat_layer,
    vectors,
):
    pieces = (
        in_layer[0, 0].astype(jnp.bfloat16),
        mid_layer[0, 0].astype(jnp.bfloat16),
        feat_layer[0, 0].astype(jnp.bfloat16),
        vectors[0, 0].astype(jnp.bfloat16),
    )
    weights = (
        lax.all_gather(pieces[0], "rays", axis=0, tiled=True),
        lax.all_gather(pieces[1], "rays", axis=0, tiled=True),
        lax.all_gather(pieces[2], "rays", axis=0, tiled=True),
        lax.all_gather(pieces[3], "rays", axis=0, tiled=True),
    )
    regions = lax.axis_size("region")
    found = forward(
        ray_codes, depth_bins[0], entries[0], exits[0], weights, depth_scale / (regions * BINS)
    )
    colour, optical, local_weight = (found[4], found[5], found[7])
    depth = jnp.sum(optical, 0)
    local_partial = jnp.sum(local_weight[:, :, None] * colour, 0)
    onward = direction == 0
    nothing = jnp.zeros_like(depth)
    below_depth = entering(depth, "region", jnp.add, nothing, False)
    above_depth = entering(depth, "region", jnp.add, nothing, True)
    entry_trans = jnp.exp(-jnp.where(onward, below_depth, above_depth))
    contribution = entry_trans[:, None] * local_partial
    rendered = lax.psum(contribution, "region")
    feature_grad = (rendered - target.astype(jnp.float32)).astype(jnp.bfloat16)
    region_grad = entry_trans * jnp.sum(feature_grad.astype(jnp.float32) * local_partial, -1)
    below_grad = entering(region_grad, "region", jnp.add, nothing, False)
    above_grad = entering(region_grad, "region", jnp.add, nothing, True)
    after_sum = jnp.where(onward, above_grad, below_grad)
    in_grad, mid_grad, feat_grad, vec_grad = backward(
        found, weights, entry_trans, after_sum, feature_grad
    )
    in_share, mid_share, feat_share, vec_share = (
        lax.psum_scatter(in_grad, "rays", scatter_dimension=0, tiled=True),
        lax.psum_scatter(mid_grad, "rays", scatter_dimension=0, tiled=True),
        lax.psum_scatter(feat_grad, "rays", scatter_dimension=0, tiled=True),
        lax.psum_scatter(vec_grad, "rays", scatter_dimension=0, tiled=True),
    )
    return (
        adam_update(in_layer[:, 0], in_share)[:, None],
        adam_update(mid_layer[:, 0], mid_share)[:, None],
        adam_update(feat_layer[:, 0], feat_share)[:, None],
        adam_update(vectors[:, 0], vec_share)[:, None],
        (-after_sum)[None],
    )


def solution(mesh):
    placed = (
        P(None, "rays", None),
        P("rays", None),
        P("rays"),
        P("region", "rays"),
        P("region", "rays"),
        P("region", None, "rays"),
        P(None, "region", "rays", None),
        P(None, "region", "rays", None),
        P(None, "region", "rays", None),
        P(None, "region", "rays"),
    )
    return jax.shard_map(
        per_device,
        mesh=mesh,
        in_specs=placed,
        out_specs=(
            P(None, "region", "rays", None),
            P(None, "region", "rays", None),
            P(None, "region", "rays", None),
            P(None, "region", "rays"),
            P("region", "rays"),
        ),
        check_vma=False,
    )
```

profile of v0, /device:TPU:1, one launch (start us, length us, event | category | flops | bytes accessed | tf_op | source)
XLA Modules:
  0.0 704.3 jit_solution(14926614243733913002)
XLA Ops:
  12.2 18.6 %all-reduce.1 = bf16[1152]{0:T(1024)(128)(2,1)S(1)} all-reduce(bf16[1152]{0:T(1024)(128)(2,1)S(1)} %dynamic-update-slice), channel_id=1, replica_groups=mesh['region'=64,'rays'=8] {'rays'}, use_global_device_ids=true, to_apply=%add.1 | all-reduce | flops 1152 | bytes 4608
  33.2 13.2 %all_gather.28 = bf16[128,256]{1,0:T(8,128)(2,1)S(1)} all-gather(bf16[16,256]{1,0:T(8,128)(2,1)S(1)} %bitcast_convert_fusion.2), channel_id=1, replica_groups=mesh['region'=64,'rays'=8] {'rays'}, dimensions={0}, use_global_device_ids=true | all-gather | bytes 73728 | tf_op jit(solution)/shard_map/all_gather | solution.py:169
  47.1 12.7 %all_gather.30 = bf16[256,256]{1,0:T(8,128)(2,1)S(1)} all-gather(bf16[32,256]{1,0:T(8,128)(2,1)S(1)} %bitcast_convert_fusion.1), channel_id=1, replica_groups=mesh['region'=64,'rays'=8] {'rays'}, dimensions={0}, use_global_device_ids=true | all-gather | bytes 147456 | tf_op jit(solution)/shard_map/all_gather | solution.py:170
  63.7 77.3 %all-gather.2 = f32[64,1,512]{2,1,0:T(1,128)S(1)} all-gather(f32[1,1,512]{2,1,0:T(1,128)S(1)} %bitcast.202), channel_id=2, replica_groups=mesh['region'=64,'rays'=8] {'region'}, dimensions={0}, use_global_device_ids=true | all-gather | bytes 133120 | tf_op jit(solution)/shard_map/all_gather | solution.py:20
  141.1 3.6 while.56
  144.7 3.6 while.57
  148.4 39.0 %all_gather.33 = bf16[256,384]{1,0:T(8,128)(2,1)S(1)} all-gather(bf16[32,384]{1,0:T(8,128)(2,1)S(1)} %bitcast_convert_fusion), channel_id=1, replica_groups=mesh['region'=64,'rays'=8] {'rays'}, dimensions={0}, use_global_device_ids=true | all-gather | bytes 221184 | tf_op jit(solution)/shard_map/all_gather | solution.py:171
  188.6 1.8 add_divide_fusion
  191.2 1.8 copy-done
  195.6 254.0 %all-reduce.5.cloned.1.call-done = f32[512,384]{1,0:T(8,128)} async-done(((f32[512,384]{1,0:T(8,128)}), f32[512,384]{1,0:T(8,128)}) %all-reduce.5.cloned.1.call-update) | async-done | bytes 786448 | tf_op jit(solution)/shard_map/psum | solution.py:187
  449.6 1.9 multiply_reduce_fusion.1
  451.5 5.1 convert_reduce_fusion
  456.9 72.2 %all-gather.3 = f32[64,1,512]{2,1,0:T(1,128)S(1)} all-gather(f32[1,1,512]{2,1,0:T(1,128)S(1)} %bitcast.203), channel_id=3, replica_groups=mesh['region'=64,'rays'=8] {'region'}, dimensions={0}, use_global_device_ids=true | all-gather | bytes 133120 | tf_op jit(solution)/shard_map/all_gather | solution.py:20
  529.3 3.6 while.58
  532.9 3.6 while.59
  537.2 3.3 convert_reduce_fusion.1
  540.6 2.3 convert_reduce_fusion.2
  542.9 1.5 fusion.40
  544.3 2.8 fusion.39
  547.9 48.9 %all-reduce.2 = f32[1152]{0:T(1024)S(1)} all-reduce(f32[1152]{0:T(1024)S(1)} %pad_maximum_fusion), channel_id=7, replica_groups=mesh['region'=64,'rays'=8] {'rays'}, use_global_device_ids=true, to_apply=%region_21.22.clone | all-reduce | flops 1152 | bytes 9216
  596.9 4.0 fusion.41
  601.6 14.0 %reduce-scatter.4.cloned.1.call-done = f32[16,256]{1,0:T(8,128)} async-done(((f32[128,256]{1,0:T(8,128)}), f32[16,256]{1,0:T(8,128)}) %reduce-scatter.4.cloned.1.call-update) | async-done | bytes 16400 | tf_op jit(solution)/shard_map/reduce_scatter | solution.py:197
  617.0 38.9 %reduce-scatter.6.cloned.1.call-done = f32[32,256]{1,0:T(8,128)} async-done(((f32[256,256]{1,0:T(8,128)}), f32[32,256]{1,0:T(8,128)}) %reduce-scatter.6.cloned.1.call-update) | async-done | bytes 32784 | tf_op jit(solution)/shard_map/reduce_scatter | solution.py:198
  657.4 38.8 %reduce-scatter.8.cloned.1.call-done = f32[32,384]{1,0:T(8,128)} async-done(((f32[256,384]{1,0:T(8,128)}), f32[32,384]{1,0:T(8,128)}) %reduce-scatter.8.cloned.1.call-update) | async-done | bytes 49168 | tf_op jit(solution)/shard_map/reduce_scatter | solution.py:199
  (620 shorter events, 27.6 us)
Async XLA Ops:
  7.2 442.5 %all-reduce.5.cloned.1.call-start = ((), (), s32[]{:S(2)}) async-start(), calls=%async_computation.3 | async-start | bytes 1572864 | tf_op jit(solution)/shard_map/psum | solution.py:187
  10.0 2.0 copy-start.17
  59.9 2.5 copy-start.9
  61.6 2.0 copy-start.13
  62.9 85.5 %copy-start.5 = (f32[3,1,32,384]{3,2,1,0:T(8,128)S(1)}, f32[3,1,32,384]{3,2,1,0:T(8,128)}, u32[]{:S(2)}) copy-start(f32[3,1,32,384]{3,2,1,0:T(8,128)} %param.26) | copy-start | bytes 442372
  62.9 124.5 %copy-start.20 = (s32[512]{0:T(512)S(1)}, s32[512]{0:T(512)}, u32[]{:S(2)}) copy-start(s32[512]{0:T(512)} %param.20) | copy-start | bytes 6148
  187.4 3.0 copy-start.6
  190.4 2.7 copy-start
  190.4 259.2 %copy-start.3 = (bf16[512,384]{1,0:T(8,128)(2,1)S(1)}, bf16[512,384]{1,0:T(8,128)(2,1)}, u32[]{:S(2)}) copy-start(bf16[512,384]{1,0:T(8,128)(2,1)} %param.19) | copy-start | bytes 1179652
  194.1 421.5 %reduce-scatter.4.cloned.1.call-start = ((), (), s32[]{:S(2)}) async-start(), calls=%async_computation.4 | async-start | bytes 147456 | tf_op jit(solution)/shard_map/reduce_scatter | solution.py:197
  451.5 5.3 copy-start.15
  451.5 85.0 %copy-start.21 = (pred[512]{0:T(512)(128)(4,1)S(1)}, pred[512]{0:T(512)(128)(4,1)}, u32[]{:S(2)}) copy-start(pred[512]{0:T(512)(128)(4,1)} %get-tuple-element.439) | copy-start | bytes 1540
  451.5 85.6 %copy-start.14 = (s32[1,512]{1,0:T(1,128)S(1)}, s32[1,512]{1,0:T(1,128)}, u32[]{:S(2)}) copy-start(s32[1,512]{1,0:T(1,128)} %param.21) | copy-start | bytes 6148
  451.5 85.7 %copy-start.7 = (bf16[256,384]{1,0:T(8,128)(2,1)S(1)}, bf16[256,384]{1,0:T(8,128)(2,1)}, u32[]{:S(2)}) copy-start(bf16[256,384]{1,0:T(8,128)(2,1)} %copy-done.6) | copy-start | bytes 589828
  451.5 85.7 %copy-start.22 = (f32[256]{0:T(256)S(1)}, f32[256]{0:T(256)}, u32[]{:S(2)}) copy-start(f32[256]{0:T(256)} %get-tuple-element.454) | copy-start | bytes 3076
  537.2 3.4 copy-start.10
  537.2 3.4 copy-start.24
  547.1 108.8 %reduce-scatter.6.cloned.1.call-start = ((), (), s32[]{:S(2)}) async-start(), calls=%async_computation.5 | async-start | bytes 294912 | tf_op jit(solution)/shard_map/reduce_scatter | solution.py:198
  547.9 148.3 %reduce-scatter.8.cloned.1.call-start = ((), (), s32[]{:S(2)}) async-start(), calls=%async_computation.6 | async-start | bytes 442368 | tf_op jit(solution)/shard_map/reduce_scatter | solution.py:199
  596.9 4.0 copy-start.16
  596.9 4.0 copy-start.18
  596.9 4.0 copy-start.19
  596.9 18.8 %copy-start.11 = (f32[3,1,16,256]{3,2,1,0:T(8,128)S(1)}, f32[3,1,16,256]{3,2,1,0:T(8,128)}, u32[]{:S(2)}) copy-start(f32[3,1,16,256]{3,2,1,0:T(8,128)} %param.24) | copy-start | bytes 147460
  596.9 59.1 %copy-start.8 = (f32[3,1,32,256]{3,2,1,0:T(8,128)S(1)}, f32[3,1,32,256]{3,2,1,0:T(8,128)}, u32[]{:S(2)}) copy-start(f32[3,1,32,256]{3,2,1,0:T(8,128)} %param.25) | copy-start | bytes 294916
  (5 other events, 7.7 us)
Sparse Core Ops, SparseCore 0:
  194.3 255.3 all-reduce.4
  547.2 68.3 reduce-scatter.3
  618.5 37.4 reduce-scatter.5
  658.6 37.5 reduce-scatter.7
where the time goes:
time: 706 us; the launch traced here: 704 us
  waiting for transfers between devices  346 us (49%)
  blocking collectives  282 us (40%)
  other arithmetic  23.3 us (3%)
  matrix products  18 us (3%)
  between operations  15.6 us (2%)
  local copies, waits for them, and re-layouts  10.3 us (1%)
  loops' own time  8.82 us (1%)
    psum x1, waiting for transfers between devices, per_device(): rendered = lax.psum(contribution, 'region')  254 us
    all_gather x2, blocking collectives, entering(): pieces = lax.all_gather(value, axis)  150 us
    unnamed x2, blocking collectives  67.5 us
    all_gather x1, blocking collectives, per_device(): lax.all_gather(pieces[2], 'rays', axis=0, tiled=True)  39 us
    reduce_scatter x1, waiting for transfers between devices, per_device(): lax.psum_scatter(mid_grad, 'rays', scatter_dimension=0, tiled=True)  38.9 us
    reduce_scatter x1, waiting for transfers between devices, per_device(): lax.psum_scatter(feat_grad, 'rays', scatter_dimension=0, tiled=True)  38.8 us
  transfers between devices with their start and end apart: 4, of which 4 were waited for; matrix products, arithmetic and copies ran while one was open for 1% of the time, Pallas kernels for 0%

commit v1 on v0

--- a/solution.py
+++ b/solution.py
@@ -1,6 +1,8 @@
 import jax
 import jax.numpy as jnp
 from jax import lax
+from jax.experimental import pallas as pl
+from jax.experimental.pallas import tpu as pltpu
 from jax.sharding import PartitionSpec as P
 
 BINS = 64
@@ -13,21 +15,6 @@
 epsilon = 1e-08
 first_fix = 1.0 - 0.9**10
 second_fix = 1.0 - 0.999**10
-
-
-def entering(value, axis, join, neutral, backward):
-    count, mine = (lax.axis_size(axis), lax.axis_index(axis))
-    pieces = lax.all_gather(value, axis)
-    if backward:
-        pieces = pieces[::-1]
-        mine = count - 1 - mine
-    total = jnp.full_like(value, 0) + jnp.asarray(neutral, value.dtype)
-
-    def lap(position, total):
-        longer = join(total, pieces[position])
-        return jnp.where(position < mine, longer, total)
-
-    return lax.fori_loop(0, count - 1, lap, total)
 
 
 def forward(ray_codes, depth_bins, entry_row, exit_row, weights, unit_length):
@@ -147,6 +134,358 @@
     return jnp.stack([stacked[0] - learn_rate * update_step, first_moment, second])
 
 
+MESH = pl.DeviceIdType.MESH
+NX = 4
+NZ = 16
+NR = 8
+RX = 128
+RZ = 8
+FEAT = 384
+
+
+def vmem(count):
+    return [pl.BlockSpec(memory_space=pltpu.VMEM)] * count
+
+
+def remote(source, target, send_sem, recv_sem, peer):
+    return pltpu.make_async_remote_copy(
+        src_ref=source,
+        dst_ref=target,
+        send_sem=send_sem,
+        recv_sem=recv_sem,
+        device_id=peer,
+        device_id_type=MESH,
+    )
+
+
+def gather_kernel(
+    in_ref, mid_ref, feat_ref, vec_ref, in_out, mid_out, feat_out, vec_out, send_sem, recv_sem
+):
+    me = lax.axis_index("rays")
+    in_out[me] = in_ref[...].astype(jnp.bfloat16)
+    mid_out[me] = mid_ref[...].astype(jnp.bfloat16)
+    feat_out[me] = feat_ref[...].astype(jnp.bfloat16)
+    vec_out[me] = vec_ref[...].astype(jnp.bfloat16).astype(jnp.float32)
+    barrier = pltpu.get_barrier_semaphore()
+    for step in range(1, NR):
+        pl.semaphore_signal(
+            barrier, inc=1, device_id={"rays": lax.rem(me + step, NR)}, device_id_type=MESH
+        )
+    pl.semaphore_wait(barrier, NR - 1)
+    outs = (in_out, mid_out, feat_out, vec_out)
+    for kind, out in enumerate(outs):
+        for step in range(1, NR):
+            peer = lax.rem(me + step, NR)
+            remote(
+                out.at[me],
+                out.at[me],
+                send_sem.at[kind, step],
+                recv_sem.at[kind, step],
+                {"rays": peer},
+            ).start()
+    for kind, out in enumerate(outs):
+        for step in range(1, NR):
+            origin = lax.rem(me + NR - step, NR)
+            remote(
+                out.at[origin],
+                out.at[origin],
+                send_sem.at[kind, step],
+                recv_sem.at[kind, step],
+                {"rays": origin},
+            ).wait()
+
+
+def gather_weights(in_part, mid_part, feat_part, vec_part):
+    shapes = (
+        jax.ShapeDtypeStruct((NR, 16, 256), jnp.bfloat16),
+        jax.ShapeDtypeStruct((NR, 32, 256), jnp.bfloat16),
+        jax.ShapeDtypeStruct((NR, 32, 384), jnp.bfloat16),
+        jax.ShapeDtypeStruct((NR, 1, 144), jnp.float32),
+    )
+    return pl.pallas_call(
+        gather_kernel,
+        out_shape=shapes,
+        in_specs=vmem(4),
+        out_specs=tuple(vmem(4)),
+        scratch_shapes=[pltpu.SemaphoreType.DMA((4, NR)), pltpu.SemaphoreType.DMA((4, NR))],
+        compiler_params=pltpu.CompilerParams(collective_id=0, has_side_effects=True),
+        name="gather_weights",
+    )(in_part, mid_part, feat_part, vec_part)
+
+
+def far_first(count):
+    half = count // 2
+    order = [half]
+    for gap in range(1, half):
+        order += [half - gap, half + gap]
+    return order
+
+
+def ordered_sums(table, own_z):
+    column = jnp.zeros((NX, 1, RX), jnp.float32)
+    lower = jnp.zeros((NX, 1, RX), jnp.float32)
+    upper = jnp.zeros((NX, 1, RX), jnp.float32)
+    for z in range(NZ):
+        rows = table[z]
+        column = column + rows
+        lower = lower + rows * (z < own_z).astype(jnp.float32)
+        upper = upper + rows * (z > own_z).astype(jnp.float32)
+    below, above = [], []
+    for x in range(NX):
+        under, over = lower[x], upper[x]
+        for other in range(NX):
+            if other < x:
+                under = under + column[other]
+            if other > x:
+                over = over + column[other]
+        below.append(under)
+        above.append(over)
+    return below, above
+
+
+def region_kernel(
+    partial_ref,
+    depth_ref,
+    onward_ref,
+    target_ref,
+    trans_out,
+    after_out,
+    grad_out,
+    partial_x,
+    depth_z,
+    pieces,
+    pieces_z,
+    grad_z,
+    region_z,
+    trans_send,
+    after_send,
+    sem_partial,
+    sem_depth,
+    sem_depth_z,
+    sem_piece,
+    sem_grad_z,
+    sem_region,
+    sem_trans,
+    sem_grad,
+    sem_after,
+):
+    place = lax.axis_index("region")
+    own_x, own_z = place // NZ, lax.rem(place, NZ)
+
+    def along_x(step):
+        return lax.rem(own_x + step, NX)
+
+    def along_z(step):
+        return lax.rem(own_z + step, NZ)
+
+    def at(x, z):
+        return {"region": x * NZ + z}
+
+    barrier = pltpu.get_barrier_semaphore()
+    for step in range(1, NZ):
+        pl.semaphore_signal(
+            barrier, inc=1, device_id=at(own_x, along_z(step)), device_id_type=MESH
+        )
+    for step in range(1, NX):
+        pl.semaphore_signal(
+            barrier, inc=1, device_id=at(along_x(step), own_z), device_id_type=MESH
+        )
+    pl.semaphore_wait(barrier, NX + NZ - 2)
+
+    def spread_x(source, target, sems):
+        for step in (2, 1, 3):
+            x = along_x(step)
+            remote(
+                source(x), target.at[own_x], sems.at[0, step], sems.at[1, step], at(x, own_z)
+            ).start()
+
+    def wait_x(source, target, sems):
+        for step in (1, 3, 2):
+            x = along_x(NX - step)
+            remote(source(x), target.at[x], sems.at[0, step], sems.at[1, step], at(x, own_z)).wait()
+
+    def spread_z(source, target, sems):
+        for step in far_first(NZ):
+            z = along_z(step)
+            remote(
+                source(z), target.at[own_z], sems.at[0, step], sems.at[1, step], at(own_x, z)
+            ).start()
+
+    def wait_z(source, target, sems):
+        for step in far_first(NZ)[::-1]:
+            z = along_z(NZ - step)
+            remote(source(z), target.at[z], sems.at[0, step], sems.at[1, step], at(own_x, z)).wait()
+
+    depth_own = depth_z.at[own_z]
+    depth_own[own_x] = depth_ref[own_x]
+    spread_x(lambda x: depth_ref.at[x], depth_own, sem_depth)
+    spread_x(lambda x: partial_ref.at[x], partial_x, sem_partial)
+    partial_x[own_x] = partial_ref[own_x]
+    wait_x(lambda x: depth_ref.at[x], depth_own, sem_depth)
+    spread_z(lambda z: depth_own, depth_z, sem_depth_z)
+    wait_z(lambda z: depth_own, depth_z, sem_depth_z)
+    below, above = ordered_sums(depth_z, own_z)
+    onward = onward_ref[own_x] == 0
+    filler = jnp.zeros((RX - NX, RX), jnp.float32)
+    trans = [jnp.exp(-jnp.where(onward, below[x], above[x])) for x in range(NX)]
+    for x in range(NX):
+        trans_send[x] = trans[x]
+    trans_out[own_x] = trans_send[own_x]
+    spread_x(lambda x: trans_send.at[x], trans_out, sem_trans)
+    columns = jnp.transpose(jnp.concatenate(trans + [filler], 0))
+    wait_x(lambda x: partial_ref.at[x], partial_x, sem_partial)
+    total = jnp.zeros((RX, FEAT), jnp.float32)
+    for x in range(NX):
+        total = total + columns[:, x : x + 1] * partial_x[x].astype(jnp.float32)
+    pieces[...] = total.reshape(NZ, RZ, FEAT).astype(jnp.bfloat16)
+    spread_z(lambda z: pieces.at[z], pieces_z, sem_piece)
+    pieces_z[own_z] = pieces[own_z]
+    first = pl.multiple_of(own_x * RX + (own_z // 2) * (2 * RZ), 2 * RZ)
+    wanted = target_ref[pl.ds(first, 2 * RZ), :].astype(jnp.float32)
+    odd = (lax.rem(own_z, 2)).astype(jnp.float32)
+    wanted = wanted[:RZ] * (1.0 - odd) + wanted[RZ:] * odd
+    wait_z(lambda z: pieces.at[z], pieces_z, sem_piece)
+    rendered = jnp.sum(pieces_z[...].astype(jnp.float32), 0)
+    grad_z[own_z] = (rendered - wanted).astype(jnp.bfloat16)
+    spread_z(lambda z: grad_z.at[own_z], grad_z, sem_grad_z)
+    wait_z(lambda z: grad_z.at[own_z], grad_z, sem_grad_z)
+    grad_float = grad_z[...].astype(jnp.float32).reshape(RX, FEAT)
+    grad_out[own_x] = grad_float.astype(jnp.bfloat16)
+    dots = [
+        jnp.sum(grad_float * partial_x[x].astype(jnp.float32), -1, keepdims=True)
+        for x in range(NX)
+    ]
+    lane = lax.broadcasted_iota(jnp.int32, (RX, RX), 1)
+    grid = jnp.zeros((RX, RX), jnp.float32)
+    for x in range(NX):
+        grid = jnp.where(lane == x, dots[x], grid)
+    grid = jnp.transpose(grid)
+    region_own = region_z.at[own_z]
+    for x in range(NX):
+        region_own[x] = grid[x : x + 1] * trans_send[x]
+    spread_z(lambda z: region_own, region_z, sem_region)
+    spread_x(lambda x: grad_out.at[own_x], grad_out, sem_grad)
+    wait_z(lambda z: region_own, region_z, sem_region)
+    below, above = ordered_sums(region_z, own_z)
+    for x in range(NX):
+        after_send[x] = jnp.where(onward, above[x], below[x])
+    after_out[own_x] = after_send[own_x]
+    spread_x(lambda x: after_send.at[x], after_out, sem_after)
+    wait_x(lambda x: trans_send.at[x], trans_out, sem_trans)
+    wait_x(lambda x: grad_out.at[own_x], grad_out, sem_grad)
+    wait_x(lambda x: after_send.at[x], after_out, sem_after)
+
+
+def exchange_regions(partial, depth, direction, target):
+    row = jax.ShapeDtypeStruct((NX, 1, RX), jnp.float32)
+    return pl.pallas_call(
+        region_kernel,
+        out_shape=(row, row, jax.ShapeDtypeStruct((NX, RX, FEAT), jnp.bfloat16)),
+        in_specs=vmem(4),
+        out_specs=tuple(vmem(3)),
+        scratch_shapes=[
+            pltpu.VMEM((NX, RX, FEAT), jnp.bfloat16),
+            pltpu.VMEM((NZ, NX, 1, RX), jnp.float32),
+            pltpu.VMEM((NZ, RZ, FEAT), jnp.bfloat16),
+            pltpu.VMEM((NZ, RZ, FEAT), jnp.bfloat16),
+            pltpu.VMEM((NZ, RZ, FEAT), jnp.bfloat16),
+            pltpu.VMEM((NZ, NX, 1, RX), jnp.float32),
+            pltpu.VMEM((NX, 1, RX), jnp.float32),
+            pltpu.VMEM((NX, 1, RX), jnp.float32),
+            pltpu.SemaphoreType.DMA((2, NX)),
+            pltpu.SemaphoreType.DMA((2, NX)),
+            pltpu.SemaphoreType.DMA((2, NZ)),
+            pltpu.SemaphoreType.DMA((2, NZ)),
+            pltpu.SemaphoreType.DMA((2, NZ)),
+            pltpu.SemaphoreType.DMA((2, NZ)),
+            pltpu.SemaphoreType.DMA((2, NX)),
+            pltpu.SemaphoreType.DMA((2, NX)),
+            pltpu.SemaphoreType.DMA((2, NX)),
+        ],
+        compiler_params=pltpu.CompilerParams(collective_id=1, has_side_effects=True),
+        name="exchange_regions",
+    )(partial, depth, direction, target)
+
+
+def reduce_kernel(
+    in_ref,
+    mid_ref,
+    feat_ref,
+    vec_ref,
+    in_out,
+    mid_out,
+    feat_out,
+    vec_out,
+    in_send,
+    mid_send,
+    feat_send,
+    in_got,
+    mid_got,
+    feat_got,
+    vec_got,
+    send_sem,
+    recv_sem,
+):
+    me = lax.axis_index("rays")
+    feat_send[...] = feat_ref[...].astype(jnp.bfloat16)
+    mid_send[...] = mid_ref[...].astype(jnp.bfloat16)
+    in_send[...] = in_ref[...].astype(jnp.bfloat16)
+    barrier = pltpu.get_barrier_semaphore()
+    for step in range(1, NR):
+        pl.semaphore_signal(
+            barrier, inc=1, device_id={"rays": lax.rem(me + step, NR)}, device_id_type=MESH
+        )
+    pl.semaphore_wait(barrier, NR - 1)
+    moves = (
+        (feat_send, feat_got, feat_ref, feat_out),
+        (mid_send, mid_got, mid_ref, mid_out),
+        (in_send, in_got, in_ref, in_out),
+        (vec_ref, vec_got, vec_ref, vec_out),
+    )
+    for kind, (source, got, _, _) in enumerate(moves):
+        for step in range(1, NR):
+            peer = lax.rem(me + step, NR)
+            remote(
+                source.at[peer],
+                got.at[step],
+                send_sem.at[kind, step],
+                recv_sem.at[kind, step],
+                {"rays": peer},
+            ).start()
+    for kind, (source, got, own, out) in enumerate(moves):
+        total = own[me]
+        for step in range(1, NR):
+            origin = lax.rem(me + NR - step, NR)
+            remote(
+                source.at[origin],
+                got.at[step],
+                send_sem.at[kind, step],
+                recv_sem.at[kind, step],
+                {"rays": origin},
+            ).wait()
+            total = total + got[step].astype(jnp.float32)
+        out[...] = total
+
+
+def reduce_grads(in_grad, mid_grad, feat_grad, vec_grad):
+    shapes = ((16, 256), (32, 256), (32, 384), (1, 144))
+    return pl.pallas_call(
+        reduce_kernel,
+        out_shape=tuple(jax.ShapeDtypeStruct(shape, jnp.float32) for shape in shapes),
+        in_specs=vmem(4),
+        out_specs=tuple(vmem(4)),
+        scratch_shapes=[pltpu.VMEM((NR,) + shape, jnp.bfloat16) for shape in shapes[:3]]
+        + [pltpu.VMEM((NR,) + shape, jnp.bfloat16) for shape in shapes[:3]]
+        + [
+            pltpu.VMEM((NR, 1, 144), jnp.float32),
+            pltpu.SemaphoreType.DMA((4, NR)),
+            pltpu.SemaphoreType.DMA((4, NR)),
+        ],
+        compiler_params=pltpu.CompilerParams(collective_id=2, has_side_effects=True),
+        name="reduce_grads",
+    )(in_grad, mid_grad, feat_grad, vec_grad)
+
+
 def per_device(
     ray_codes,
     target,
@@ -159,17 +498,14 @@
     feat_layer,
     vectors,
 ):
-    pieces = (
-        in_layer[0, 0].astype(jnp.bfloat16),
-        mid_layer[0, 0].astype(jnp.bfloat16),
-        feat_layer[0, 0].astype(jnp.bfloat16),
-        vectors[0, 0].astype(jnp.bfloat16),
+    in_all, mid_all, feat_all, vec_all = gather_weights(
+        in_layer[0, 0], mid_layer[0, 0], feat_layer[0, 0], vectors[0]
     )
     weights = (
-        lax.all_gather(pieces[0], "rays", axis=0, tiled=True),
-        lax.all_gather(pieces[1], "rays", axis=0, tiled=True),
-        lax.all_gather(pieces[2], "rays", axis=0, tiled=True),
-        lax.all_gather(pieces[3], "rays", axis=0, tiled=True),
+        in_all.reshape(128, 256),
+        mid_all.reshape(256, 256),
+        feat_all.reshape(256, 384),
+        vec_all.reshape(1152).astype(jnp.bfloat16),
     )
     regions = lax.axis_size("region")
     found = forward(
@@ -178,32 +514,28 @@
     colour, optical, local_weight = (found[4], found[5], found[7])
     depth = jnp.sum(optical, 0)
     local_partial = jnp.sum(local_weight[:, :, None] * colour, 0)
-    onward = direction == 0
-    nothing = jnp.zeros_like(depth)
-    below_depth = entering(depth, "region", jnp.add, nothing, False)
-    above_depth = entering(depth, "region", jnp.add, nothing, True)
-    entry_trans = jnp.exp(-jnp.where(onward, below_depth, above_depth))
-    contribution = entry_trans[:, None] * local_partial
-    rendered = lax.psum(contribution, "region")
-    feature_grad = (rendered - target.astype(jnp.float32)).astype(jnp.bfloat16)
-    region_grad = entry_trans * jnp.sum(feature_grad.astype(jnp.float32) * local_partial, -1)
-    below_grad = entering(region_grad, "region", jnp.add, nothing, False)
-    above_grad = entering(region_grad, "region", jnp.add, nothing, True)
-    after_sum = jnp.where(onward, above_grad, below_grad)
+    entry_trans, after_sum, feature_grad = exchange_regions(
+        local_partial.astype(jnp.bfloat16).reshape(NX, RX, FEAT),
+        depth.reshape(NX, 1, RX),
+        direction.reshape(NX, 1, RX),
+        target,
+    )
+    entry_trans, after_sum = entry_trans.reshape(-1), after_sum.reshape(-1)
+    feature_grad = feature_grad.reshape(NX * RX, FEAT)
     in_grad, mid_grad, feat_grad, vec_grad = backward(
         found, weights, entry_trans, after_sum, feature_grad
     )
-    in_share, mid_share, feat_share, vec_share = (
-        lax.psum_scatter(in_grad, "rays", scatter_dimension=0, tiled=True),
-        lax.psum_scatter(mid_grad, "rays", scatter_dimension=0, tiled=True),
-        lax.psum_scatter(feat_grad, "rays", scatter_dimension=0, tiled=True),
-        lax.psum_scatter(vec_grad, "rays", scatter_dimension=0, tiled=True),
+    in_share, mid_share, feat_share, vec_share = reduce_grads(
+        in_grad.reshape(NR, 16, 256),
+        mid_grad.reshape(NR, 32, 256),
+        feat_grad.reshape(NR, 32, 384),
+        vec_grad.reshape(NR, 1, 144),
     )
     return (
         adam_update(in_layer[:, 0], in_share)[:, None],
         adam_update(mid_layer[:, 0], mid_share)[:, None],
         adam_update(feat_layer[:, 0], feat_share)[:, None],
-        adam_update(vectors[:, 0], vec_share)[:, None],
+        adam_update(vectors[:, 0], vec_share[0])[:, None],
         (-after_sum)[None],
     )
 

time: 706 us -> 133 us (0.19)
  waiting for transfers between devices: 346 us -> 0 us
  blocking collectives: 282 us -> 0 us
  Pallas kernels: 0 us -> 79.5 us
  between operations: 15.6 us -> 1.06 us
  loops' own time: 8.82 us -> 0 us
    psum x1 -> x0, waiting for transfers between devices: 254 us -> none  [per_device(): rendered = lax.psum(contribution, 'region')]
    all_gather x5 -> x0, blocking collectives: 215 us -> none  [the longest x2 150 us: entering(): pieces = lax.all_gather(value, axis)]
    reduce_scatter x3 -> x0, waiting for transfers between devices: 91.7 us -> none  [the longest x1 38.9 us: per_device(): lax.psum_scatter(mid_grad, 'rays', scatter_dimension=0, tiled=True)]
    pallas_call x0 -> x3, Pallas kernels: none -> 79.5 us  [the longest x1 44.4 us: exchange_regions(): pl.pallas_call(region_kernel, out_shape=(row, row, jax.ShapeDtypeStruct((...]
    unnamed x2 -> x0, blocking collectives: 67.5 us -> none
    another operation x4 -> x0, loops' own time: 8.82 us -> none  [entering(): return lax.fori_loop(0, count - 1, lap, total)]
  transfers between devices with their start and end apart: 4 -> 0, of which waited for: 4 -> 0; matrix products, arithmetic and copies ran while one was open for 1% -> 0% of each run, Pallas kernels for 0% -> 0%
where the time goes in v1:
time: 133 us; the launch traced here: 132 us
  Pallas kernels  79.5 us (60%)
  other arithmetic  17.3 us (13%)
  matrix products  17.1 us (13%)
  local copies, waits for them, and re-layouts  17 us (13%)
    pallas_call x1, Pallas kernels, exchange_regions(): pl.pallas_call(region_kernel, out_shape=(row, row, jax.ShapeDtypeStruct((...  44.4 us
    pallas_call x1, Pallas kernels, gather_weights(): pl.pallas_call(gather_kernel, out_shape=shapes, in_specs=vmem(4), out_spe...  18.1 us
    pallas_call x1, Pallas kernels, reduce_grads(): pl.pallas_call(reduce_kernel, out_shape=tuple((jax.ShapeDtypeStruct(shape...  17 us
    unnamed x46, local copies, waits for them, and re-layouts  6.98 us
    reduce_sum x1, other arithmetic, backward(): jnp.sum(colour_grad, 0, dtype=jnp.float32)  5.01 us
    dot_general x1, matrix products, backward(): jnp.dot(hidden_two.T, colour_grad, preferred_element_type=jnp.float32)  4.67 us
    dot_general x1, matrix products, backward(): jnp.dot(colour_grad, feat_weight.T, preferred_element_type=jnp.float32)  3.34 us
    convert_element_type x1, local copies, waits for them, and re-layouts, forward(): hidden_two = jnp.maximum(jnp.dot(hidden_one, mid_weight, preferred_elemen...  2.91 us

profile of v1, /device:TPU:1, one launch (start us, length us, event | category | flops | bytes accessed | tf_op | source)
XLA Modules:
  0.0 132.1 jit_solution(17343641439713030394)
XLA Ops:
  0.6 1.4 %slice_bitcast_fusion.2.feat_ref = f32[32,384]{1,0:T(8,128)} fusion(f32[3,1,32,384]{3,2,1,0:T(8,128)} %param.18), kind=kLoop, calls=%fused_computation.38 | loop fusion | bytes 98304 | tf_op jit(solution)/shard_map/squeeze | solution.py:502
  2.1 1.4 %slice_bitcast_fusion.3.mid_ref = f32[32,256]{1,0:T(8,128)} fusion(f32[3,1,32,256]{3,2,1,0:T(8,128)} %param.17), kind=kLoop, calls=%fused_computation.43 | loop fusion | bytes 65536 | tf_op jit(solution)/shard_map/squeeze | solution.py:502
  3.4 1.3 %slice_bitcast_fusion.5.in_ref = f32[16,256]{1,0:T(8,128)} fusion(f32[3,1,16,256]{3,2,1,0:T(8,128)} %param.16), kind=kLoop, calls=%fused_computation.61 | loop fusion | bytes 32768 | tf_op jit(solution)/shard_map/squeeze | solution.py:134
  4.8 1.2 slice_bitcast_fusion.6.vec_ref
  6.0 18.1 %gather_weights.1 = (bf16[8,16,256]{2,1,0:T(8,128)(2,1)}, bf16[8,32,256]{2,1,0:T(8,128)(2,1)}, bf16[8,32,384]{2,1,0:T(8,128)(2,1)}, f32[8,1,144]{2,1,0:T(1,128)}) custom-call(f32[16,256]{1,0:T(8,128)} %slice_bitcast_fusion.5.in_ref, f32[32,256]{1,0:T(8,128)} %slice_bitcast_fusion.3.mid_ref, f32[32,384]{1,0:T(8,128)} %slice_bitcast_fusion.2.feat_ref, ...), custom_call_target="tpu_custom_call" | custom-call | tf_op jit(solution)/shard_map/gather_weights/pallas_call | solution.py:205
  25.0 1.0 convert_element_type.107
  30.5 1.8 %add_divide_fusion = f32[4096,384]{1,0:T(8,128)S(1)} fusion(bf16[4096,256]{1,0:T(8,128)(2,1)S(1)} %fusion.10, bf16[256,384]{1,0:T(8,128)(2,1)S(1)} %bitcast.221, f32[384]{0:T(512)S(1)} %slice_convert_fusion), kind=kOutput, calls=%fused_computation.8 | convolution fusion | flops 811597824 | bytes 8586752 | tf_op jit(solution)/shard_map/dot_general | solution.py:53
  32.3 2.0 %multiply_reduce_fusion = bf16[512,384]{1,0:T(8,128)(2,1)} fusion(f32[8,512,384]{2,1,0:T(8,128)S(1)} %bitcast.191, f32[8,512]{1,0:T(8,128)S(1)} %negate_multiply_fusion), kind=kLoop, calls=%fused_computation.7 | loop fusion | flops 2949120 | bytes 6701056 | tf_op jit(solution)/shard_map/reduce_sum | solution.py:516
  34.3 0.8 copy-done
  35.0 44.4 %exchange_regions.1 = (f32[4,1,128]{2,1,0:T(1,128)}, f32[4,1,128]{2,1,0:T(1,128)}, bf16[4,128,384]{2,1,0:T(8,128)(2,1)}) custom-call(bf16[4,128,384]{2,1,0:T(8,128)(2,1)} %bitcast.200, f32[4,1,128]{2,1,0:T(1,128)} %bitcast.217, s32[4,1,128]{2,1,0:T(1,128)} %bitcast.220, bf16[512,384]{1,0:T(8,128)(2,1)} %target_ref.1), custom_call_target="tpu_custom_call" | custom-call | tf_op jit(solution)/shard_map/exchange_regions/pallas_call | solution.py:381
  80.1 1.0 convert.1
  81.1 5.0 %convert_reduce_fusion = (f32[384]{0:T(512)S(1)}, bf16[4096,384]{1,0:T(8,128)(2,1)}, f32[4096]{0:T(1024)S(1)}) fusion(f32[4096,384]{1,0:T(8,128)} %copy-done, f32[512,384]{1,0:T(8,128)S(1)} %convert.1, f32[4096]{0:T(1024)S(1)} %bitcast.206), kind=kLoop, calls=%fused_computation.6 | loop fusion | flops 14151296 | bytes 10257920 | tf_op jit(solution)/shard_map/reduce_sum | solution.py:124
  86.9 3.3 %convert_reduce_fusion.1 = (f32[256]{0:T(256)S(1)}, bf16[4096,256]{1,0:T(8,128)(2,1)S(1)}) fusion(f32[256]{0:T(256)S(1)} %get-tuple-element.56, f32[4096]{0:T(1024)S(1)} %convert_element_type.126, bf16[4096,384]{1,0:T(8,128)(2,1)} %get-tuple-element.41, bf16[256,384]{1,0:T(8,128)(2,1)S(1)} %bitcast.222, bf16[4096,256]{1,0:T(8,128)(2,1)S(1)} %fusion.10), kind=kOutput, calls=%fused_computation.20 | convolution fusion | flops 812646144 | bytes 7555072 | tf_op jit(solution)/shard_map/dot_general | solution.py:106
  90.2 2.3 %convert_reduce_fusion.2 = (f32[256]{0:T(256)S(1)}, bf16[4096,256]{1,0:T(8,128)(2,1)}) fusion(bf16[4096,256]{1,0:T(8,128)(2,1)S(1)} %get-tuple-element.61, bf16[256,256]{1,0:T(8,128)(2,1)S(1)} %bitcast.224, bf16[4096,256]{1,0:T(8,128)(2,1)S(1)} %copy-done.15), kind=kOutput, calls=%fused_computation.21 | convolution fusion | flops 542113536 | bytes 6423552 | tf_op jit(solution)/shard_map/dot_general | solution.py:113
  93.2 2.9 %copy.26 = bf16[256,4096]{1,0:T(8,128)(2,1)} copy(bf16[256,4096]{0,1:T(8,128)(2,1)S(1)} %bitcast.192) | data formatting | bytes 4194304 | tf_op jit(solution)/shard_map/convert_element_type | solution.py:48
  96.2 4.7 %fusion.11.feat_ref = f32[8,32,384]{2,1,0:T(8,128)} fusion(bf16[8,32,4096]{2,1,0:T(8,128)(2,1)} %bitcast.199, bf16[4096,384]{1,0:T(8,128)(2,1)} %get-tuple-element.41), kind=kOutput, calls=%fused_computation.22 | convolution fusion | flops 805306368 | bytes 5636096 | tf_op jit(solution)/shard_map/dot_general | solution.py:117
  100.8 1.4 %fusion.35 = f32[256,256]{1,0:T(8,128)} fusion(bf16[4096,256]{1,0:T(8,128)(2,1)S(1)} %copy-done.16, bf16[4096,256]{1,0:T(8,128)(2,1)S(1)} %copy-done.18), kind=kOutput, calls=%fused_computation.85 | convolution fusion | flops 536870912 | bytes 4456448 | tf_op jit(solution)/shard_map/dot_general | solution.py:116
  102.5 1.6 %copy.32 = f32[16,8,8,512]{3,1,2,0:T(8,128)S(1)} copy(f32[16,8,8,512]{3,2,1,0:T(8,128)S(1)} %bitcast.195) | data formatting | bytes 4194304
  104.4 1.6 %copy.34 = f32[16,8,8,512]{3,1,2,0:T(8,128)S(1)} copy(f32[16,8,8,512]{3,2,1,0:T(8,128)S(1)} %bitcast.196) | data formatting | bytes 4194304
  106.4 1.3 copy-done.1
  107.7 1.1 fusion.13.in_ref
  108.8 17.0 %reduce_grads.1 = (f32[16,256]{1,0:T(8,128)}, f32[32,256]{1,0:T(8,128)}, f32[32,384]{1,0:T(8,128)}, f32[1,144]{1,0:T(1,128)}) custom-call(f32[8,16,256]{2,1,0:T(8,128)} %fusion.13.in_ref, f32[8,32,256]{2,1,0:T(8,128)} %bitcast.203, f32[8,32,384]{2,1,0:T(8,128)} %fusion.11.feat_ref, f32[8,1,144]{2,1,0:T(1,128)} %reshape.213.vec_ref), custom_call_target="tpu_custom_call" | custom-call | tf_op jit(solution)/shard_map/reduce_grads/pallas_call | solution.py:472
  127.1 0.8 subtract_bitcast_fusion
  128.7 0.8 subtract_bitcast_fusion.1
  (83 shorter events, 12.6 us)
Async XLA Ops:
  0.6 25.7 %copy-start.2 = (s32[1,8,512]{2,1,0:T(8,128)S(1)}, s32[1,8,512]{2,1,0:T(8,128)}, u32[]{:S(2)}) copy-start(s32[1,8,512]{2,1,0:T(8,128)} %param.15) | copy-start | bytes 49156
  26.2 0.9 copy-start.13
  27.0 0.9 copy-start.12
  27.8 1.3 copy-start.14
  29.1 0.7 copy-start.6
  29.1 0.7 copy-start.7
  29.1 1.4 %copy-start.11 = (bf16[8,32,384]{2,1,0:T(8,128)(2,1)S(1)}, bf16[8,32,384]{2,1,0:T(8,128)(2,1)}, u32[]{:S(2)}) copy-start(bf16[8,32,384]{2,1,0:T(8,128)(2,1)} %get-tuple-element.19) | copy-start | bytes 589828
  32.3 2.8 %copy-start = (f32[4096,384]{1,0:T(8,128)}, f32[4096,384]{1,0:T(8,128)S(1)}, u32[]{:S(2)}) copy-start(f32[4096,384]{1,0:T(8,128)S(1)} %add_divide_fusion) | copy-start | bytes 18874372
  81.1 5.3 %copy-start.8 = (f32[4,1,128]{2,1,0:T(1,128)S(1)}, f32[4,1,128]{2,1,0:T(1,128)}, u32[]{:S(2)}) copy-start(f32[4,1,128]{2,1,0:T(1,128)} %get-tuple-element.20) | copy-start | bytes 6148
  81.1 5.3 %copy-start.9 = (f32[4,1,128]{2,1,0:T(1,128)S(1)}, f32[4,1,128]{2,1,0:T(1,128)}, u32[]{:S(2)}) copy-start(f32[4,1,128]{2,1,0:T(1,128)} %get-tuple-element.22) | copy-start | bytes 6148
  86.9 3.4 %copy-start.15 = (bf16[4096,256]{1,0:T(8,128)(2,1)S(1)}, bf16[4096,256]{1,0:T(8,128)(2,1)}, u32[]{:S(2)}) copy-start(bf16[4096,256]{1,0:T(8,128)(2,1)} %copy-done.14) | copy-start | bytes 6291460
  90.2 2.3 %copy-start.17 = (bf16[4096,256]{1,0:T(8,128)(2,1)}, bf16[4096,256]{1,0:T(8,128)(2,1)S(1)}, u32[]{:S(2)}) copy-start(bf16[4096,256]{1,0:T(8,128)(2,1)S(1)} %get-tuple-element.61) | copy-start | bytes 6291460
  96.2 4.7 %copy-start.16 = (bf16[4096,256]{1,0:T(8,128)(2,1)S(1)}, bf16[4096,256]{1,0:T(8,128)(2,1)}, u32[]{:S(2)}) copy-start(bf16[4096,256]{1,0:T(8,128)(2,1)} %copy-done.14) | copy-start | bytes 6291460
  96.2 4.7 %copy-start.18 = (bf16[4096,256]{1,0:T(8,128)(2,1)S(1)}, bf16[4096,256]{1,0:T(8,128)(2,1)}, u32[]{:S(2)}) copy-start(bf16[4096,256]{1,0:T(8,128)(2,1)} %copy-done.17) | copy-start | bytes 6291460
  106.1 1.6 %copy-start.1 = (bf16[4096,256]{1,0:T(8,128)(2,1)S(1)}, bf16[4096,256]{1,0:T(8,128)(2,1)}, u32[]{:S(2)}) copy-start(bf16[4096,256]{1,0:T(8,128)(2,1)} %get-tuple-element.63) | copy-start | bytes 6291460
  106.4 19.4 %copy-start.10 = (f32[3,1,144]{2,1,0:T(1,128)S(1)}, f32[3,1,144]{2,1,0:T(1,128)}, u32[]{:S(2)}) copy-start(f32[3,1,144]{2,1,0:T(1,128)} %param.19) | copy-start | bytes 5188
  106.4 20.7 %copy-start.3 = (f32[3,1,32,384]{3,2,1,0:T(8,128)S(1)}, f32[3,1,32,384]{3,2,1,0:T(8,128)}, u32[]{:S(2)}) copy-start(f32[3,1,32,384]{3,2,1,0:T(8,128)} %param.18) | copy-start | bytes 442372
  107.7 21.0 %copy-start.4 = (f32[3,1,32,256]{3,2,1,0:T(8,128)S(1)}, f32[3,1,32,256]{3,2,1,0:T(8,128)}, u32[]{:S(2)}) copy-start(f32[3,1,32,256]{3,2,1,0:T(8,128)} %param.17) | copy-start | bytes 294916
  107.7 22.4 %copy-start.5 = (f32[3,1,16,256]{3,2,1,0:T(8,128)S(1)}, f32[3,1,16,256]{3,2,1,0:T(8,128)}, u32[]{:S(2)}) copy-start(f32[3,1,16,256]{3,2,1,0:T(8,128)} %param.16) | copy-start | bytes 147460

commit v2 on v0

v2 whole, which is shorter than its diff:
```python
import jax
import jax.numpy as jnp
from jax import lax
from jax.experimental import pallas as pl
from jax.experimental.pallas import tpu as pltpu
from jax.sharding import PartitionSpec as P

BINS = 64


depth_scale = 4.0
beta_one = 0.9
beta_two = 0.999
learn_rate = 0.001
epsilon = 1e-08
first_fix = 1.0 - 0.9**10
second_fix = 1.0 - 0.999**10

MESH = pl.DeviceIdType.MESH
NX = 4
NZ = 16
NR = 8
RX = 128
RZ = 8
IN = 128
HID = 256
FEAT = 384
SLOTS = 8
ROWS = SLOTS * RX
PART = 144
WIDE = 256
F32 = jnp.float32
BF16 = jnp.bfloat16


def vmem(count):
    return [pl.BlockSpec(memory_space=pltpu.VMEM)] * count


def remote(source, target, send_sem, recv_sem, peer):
    return pltpu.make_async_remote_copy(
        src_ref=source,
        dst_ref=target,
        send_sem=send_sem,
        recv_sem=recv_sem,
        device_id=peer,
        device_id_type=MESH,
    )


def gather_kernel(
    in_ref,
    mid_ref,
    feat_ref,
    vec_ref,
    in_out,
    mid_out,
    feat_out,
    vec_out,
    in_own,
    mid_own,
    feat_own,
    vec_own,
    load_sem,
    send_sem,
    recv_sem,
):
    me = lax.axis_index("rays")
    barrier = pltpu.get_barrier_semaphore()
    for step in range(1, NR):
        pl.semaphore_signal(
            barrier, inc=1, device_id={"rays": lax.rem(me + step, NR)}, device_id_type=MESH
        )
    loads = (
        pltpu.make_async_copy(in_ref.at[0, 0], in_own, load_sem.at[0]),
        pltpu.make_async_copy(mid_ref.at[0, 0], mid_own, load_sem.at[1]),
        pltpu.make_async_copy(feat_ref.at[0, 0], feat_own, load_sem.at[2]),
        pltpu.make_async_copy(vec_ref.at[0], vec_own, load_sem.at[3]),
    )
    for load in loads:
        load.start()
    for load in loads:
        load.wait()
    in_out[me] = in_own[...].astype(BF16)
    mid_out[me] = mid_own[...].astype(BF16)
    feat_out[me] = feat_own[...].astype(BF16)
    vec_out[me] = jnp.zeros((1, WIDE), F32)
    vec_out[me, :, pl.ds(0, PART)] = vec_own[...].astype(BF16).astype(F32)
    pl.semaphore_wait(barrier, NR - 1)
    outs = (in_out, mid_out, vec_out, feat_out)
    for kind, out in enumerate(outs):
        for step in range(1, NR):
            peer = lax.rem(me + step, NR)
            remote(
                out.at[me],
                out.at[me],
                send_sem.at[kind, step],
                recv_sem.at[kind, step],
                {"rays": peer},
            ).start()
    for kind, out in enumerate(outs):
        for step in range(1, NR):
            origin = lax.rem(me + NR - step, NR)
            remote(
                out.at[origin],
                out.at[origin],
                send_sem.at[kind, step],
                recv_sem.at[kind, step],
                {"rays": origin},
            ).wait()


def gather_weights(in_layer, mid_layer, feat_layer, vectors):
    shapes = (
        jax.ShapeDtypeStruct((NR, 16, 256), BF16),
        jax.ShapeDtypeStruct((NR, 32, 256), BF16),
        jax.ShapeDtypeStruct((NR, 32, 384), BF16),
        jax.ShapeDtypeStruct((NR, 1, WIDE), F32),
    )
    return pl.pallas_call(
        gather_kernel,
        out_shape=shapes,
        in_specs=[pl.BlockSpec(memory_space=pl.ANY)] * 4,
        out_specs=tuple(vmem(4)),
        scratch_shapes=[
            pltpu.VMEM((16, 256), F32),
            pltpu.VMEM((32, 256), F32),
            pltpu.VMEM((32, 384), F32),
            pltpu.VMEM((1, PART), F32),
            pltpu.SemaphoreType.DMA((4,)),
            pltpu.SemaphoreType.DMA((4, NR)),
            pltpu.SemaphoreType.DMA((4, NR)),
        ],
        compiler_params=pltpu.CompilerParams(collective_id=0, has_side_effects=True),
        name="gather_weights",
    )(in_layer, mid_layer, feat_layer, vectors)


def far_first(count):
    half = count // 2
    order = [half]
    for gap in range(1, half):
        order += [half - gap, half + gap]
    return order


def z_sums(table, own_z):
    column = jnp.zeros((NX, 1, RX), F32)
    lower = jnp.zeros((NX, 1, RX), F32)
    upper = jnp.zeros((NX, 1, RX), F32)
    for z in range(NZ):
        rows = table[z]
        column = column + rows
        lower = lower + rows * (z < own_z).astype(F32)
        upper = upper + rows * (z > own_z).astype(F32)
    return column, lower, upper


def x_sums(column, lower, upper):
    below, above = [], []
    for x in range(NX):
        under, over = lower[x], upper[x]
        for other in range(NX):
            if other < x:
                under = under + column[other]
            if other > x:
                over = over + column[other]
        below.append(under)
        above.append(over)
    return below, above


def one_less_exp(value):
    series = value * (
        1.0 - value / 2.0 * (1.0 - value / 3.0 * (1.0 - value / 4.0 * (1.0 - value / 5.0)))
    )
    return jnp.where(value < 0.0625, series, 1.0 - jnp.exp(-value))


def sum_before(rows):
    running = jnp.zeros((1, RX), F32)
    found = []
    for slot in range(SLOTS):
        found.append(running)
        running = running + rows[slot : slot + 1]
    return jnp.concatenate(found, 0), running


def sum_after(rows):
    running = jnp.zeros((1, RX), F32)
    found = []
    for slot in range(SLOTS - 1, -1, -1):
        found.append(running)
        running = running + rows[slot : slot + 1]
    return jnp.concatenate(found[::-1], 0)


def to_row_groups(values):
    return jnp.sum(values.reshape(values.shape[0] // 8, 8, values.shape[1]), 0)


def dot_nt(left, right):
    return lax.dot_general(left, right, (((1,), (1,)), ((), ())), preferred_element_type=F32)


def step_kernel(
    codes_ref,
    bins_ref,
    entry_ref,
    exit_ref,
    onward_ref,
    target_ref,
    w_in,
    w_mid,
    w_feat,
    vec_ref,
    in_out,
    mid_out,
    feat_out,
    vec_out,
    after_out,
    enc,
    h1,
    h2,
    enc_t,
    h1_t,
    h2_t,
    colour,
    coef,
    cgrad,
    hgrad,
    second,
    first,
    raw_rows,
    optical_rows,
    before_rows,
    weight_rows,
    span_rows,
    sample_rows,
    dense_wide,
    vec_row,
    g_in,
    g_mid,
    g_feat,
    sum_one,
    sum_two,
    sum_dense,
    sum_feat,
    depth_z,
    stats_send,
    stats_x,
    partial_send,
    partial_x,
    trans_send,
    trans_all,
    pieces,
    pieces_z,
    grad_z,
    grad_all,
    region_z,
    after_send,
    in_send,
    mid_send,
    feat_send,
    vec_send,
    in_got,
    mid_got,
    feat_got,
    vec_got,
    sem_depth,
    sem_stats,
    sem_partial,
    sem_trans,
    sem_piece,
    sem_grad_z,
    sem_grad,
    sem_region,
    sem_after,
    sem_rays,
):
    place = lax.axis_index("region")
    me = lax.axis_index("rays")
    own_x, own_z = place // NZ, lax.rem(place, NZ)

    def along_x(step):
        return lax.rem(own_x + step, NX)

    def along_z(step):
        return lax.rem(own_z + step, NZ)

    def at(x, z):
        return {"region": x * NZ + z}

    barrier = pltpu.get_barrier_semaphore()
    for step in range(1, NZ):
        pl.semaphore_signal(
            barrier, inc=1, device_id=at(own_x, along_z(step)), device_id_type=MESH
        )
    for step in range(1, NX):
        pl.semaphore_signal(
            barrier, inc=1, device_id=at(along_x(step), own_z), device_id_type=MESH
        )
    for step in range(1, NR):
        pl.semaphore_signal(
            barrier, inc=1, device_id={"rays": lax.rem(me + step, NR)}, device_id_type=MESH
        )

    def move_x(step, source, target, sems):
        x = along_x(step)
        return remote(
            source(x), target.at[own_x], sems.at[0, step], sems.at[1, step], at(x, own_z)
        )

    def spread_x(source, target, sems):
        for step in (2, 1, 3):
            move_x(step, source, target, sems).start()

    def wait_x(source, target, sems, steps=(1, 3, 2)):
        for step in steps:
            x = along_x(NX - step)
            remote(source(x), target.at[x], sems.at[0, step], sems.at[1, step], at(x, own_z)).wait()

    def spread_z(source, target, sems):
        for step in far_first(NZ):
            z = along_z(step)
            remote(
                source(z), target.at[own_z], sems.at[0, step], sems.at[1, step], at(own_x, z)
            ).start()

    def wait_z(source, target, sems):
        for step in far_first(NZ)[::-1]:
            z = along_z(NZ - step)
            remote(source(z), target.at[z], sems.at[0, step], sems.at[1, step], at(own_x, z)).wait()

    def spread_rays(kind, source, target):
        for step in range(1, NR):
            peer = lax.rem(me + step, NR)
            remote(
                source.at[peer],
                target.at[step],
                sem_rays.at[0, kind, step],
                sem_rays.at[1, kind, step],
                {"rays": peer},
            ).start()

    def gather_rays(kind, source, target, total):
        for step in range(1, NR):
            origin = lax.rem(me + NR - step, NR)
            remote(
                source.at[origin],
                target.at[step],
                sem_rays.at[0, kind, step],
                sem_rays.at[1, kind, step],
                {"rays": origin},
            ).wait()
            total = total + target[step].astype(F32)
        return total

    unit = depth_scale / (NX * NZ * BINS)
    lane = lax.broadcasted_iota(jnp.int32, (RX, RX), 1)
    slot_row = lax.broadcasted_iota(jnp.int32, (SLOTS, RX), 0)

    row = jnp.zeros((1, 1280), F32)
    tail = jnp.zeros((1, 1280 - WIDE), F32)
    for index in range(NR):
        wide = jnp.concatenate([vec_ref[index], tail], 1)
        row = row + (pltpu.roll(wide, PART * index, 1) if index else wide)
    vec_row[...] = row
    dense_wide[...] = jnp.transpose(
        jnp.broadcast_to(row[:, 2 * HID : 3 * HID], (RX, HID))
    ).astype(BF16)
    for total in (g_in, g_mid, g_feat, sum_one, sum_two, sum_dense, sum_feat):
        total[...] = jnp.zeros(total.shape, F32)

    depth_own = depth_z.at[own_z]

    def hidden_part(index, carry):
        x = along_x(index + 1)
        lanes = pl.ds(pl.multiple_of(x * RX, RX), RX)
        bins = bins_ref[:, lanes].astype(F32)
        columns = jnp.transpose((bins + 0.5) / BINS)
        anchor = codes_ref[0, lanes, :].astype(F32)
        heading = codes_ref[1, lanes, :].astype(F32)
        for slot in range(SLOTS):
            enc[x, pl.ds(slot * RX, RX), :] = (
                anchor + columns[:, slot : slot + 1] * heading
            ).astype(BF16)
        h1[x] = jnp.maximum(
            jnp.dot(enc[x], w_in[...], preferred_element_type=F32) + vec_row[:, :HID], 0.0
        ).astype(BF16)
        h2[x] = jnp.maximum(
            jnp.dot(h1[x], w_mid[...], preferred_element_type=F32) + vec_row[:, HID : 2 * HID],
            0.0,
        ).astype(BF16)
        dense = jnp.dot(h2[x], dense_wide[...], preferred_element_type=F32)
        grid = jnp.zeros((RX, RX), F32)
        for slot in range(SLOTS):
            grid = jnp.where(lane == slot, dense[slot * RX : (slot + 1) * RX], grid)
        raw = jnp.transpose(grid)[:SLOTS]
        following = jnp.concatenate([bins[1:], jnp.full((1, RX), float(BINS), F32)], 0)
        inside = (slot_row >= entry_ref[:, lanes]) & (slot_row < exit_ref[:, lanes])
        span = jnp.where(inside, (following - bins) * unit, 0.0)
        soft = jnp.maximum(raw, 0.0) + jnp.log1p(jnp.exp(-jnp.abs(raw)))
        optical = soft * span
        before, total = sum_before(optical)
        raw_rows[x] = raw
        optical_rows[x] = optical
        before_rows[x] = before
        weight_rows[x] = jnp.exp(-before) * one_less_exp(optical)
        span_rows[x] = span
        depth_own[x] = total
        return carry

    lax.fori_loop(0, NX, hidden_part, 0)
    pl.semaphore_wait(barrier, NX + NZ + NR - 3)
    spread_z(lambda z: depth_own, depth_z, sem_depth)

    def colour_part(index, carry):
        x = along_x(index + 1)
        colour[x] = jax.nn.sigmoid(
            jnp.dot(h2[x], w_feat[...], preferred_element_type=F32)
            + vec_row[:, 3 * HID : 3 * HID + FEAT]
        )
        columns = jnp.transpose(weight_rows[x])
        local = jnp.zeros((RX, FEAT), F32)
        for slot in range(SLOTS):
            local = local + columns[:, slot : slot + 1] * colour[x, pl.ds(slot * RX, RX), :]
        partial_send[x] = local.astype(BF16)

        @pl.when(index < NX - 1)
        def _():
            move_x(index + 1, lambda x: partial_send.at[x], partial_x, sem_partial).start()

        return carry

    lax.fori_loop(0, NX, colour_part, 0)
    partial_x[own_x] = partial_send[own_x]
    wait_z(lambda z: depth_own, depth_z, sem_depth)
    column, lower, upper = z_sums(depth_z, own_z)
    for x in range(NX):
        stats_send[x, 0] = column[x]
        stats_send[x, 1] = lower[x]
        stats_send[x, 2] = upper[x]
    stats_x[own_x] = stats_send[own_x]
    spread_x(lambda x: stats_send.at[x], stats_x, sem_stats)
    wait_x(lambda x: stats_send.at[x], stats_x, sem_stats)
    below, above = x_sums(
        [stats_x[x, 0] for x in range(NX)],
        [stats_x[x, 1] for x in range(NX)],
        [stats_x[x, 2] for x in range(NX)],
    )
    onward = onward_ref[own_x] == 0
    trans = [jnp.exp(-jnp.where(onward, below[x], above[x])) for x in range(NX)]
    for x in range(NX):
        trans_send[x] = trans[x]
    trans_all[own_x] = trans_send[own_x]
    spread_x(lambda x: trans_send.at[x], trans_all, sem_trans)
    columns = jnp.transpose(jnp.concatenate(trans + trans, 0))
    wait_x(lambda x: partial_send.at[x], partial_x, sem_partial)
    total = jnp.zeros((RX, FEAT), F32)
    for x in range(NX):
        total = total + columns[:, x : x + 1] * partial_x[x].astype(F32)
    pieces[...] = total.reshape(NZ, RZ, FEAT).astype(BF16)
    spread_z(lambda z: pieces.at[z], pieces_z, sem_piece)
    pieces_z[own_z] = pieces[own_z]

    def turn_part(x, carry):
        h1_t[x] = jnp.transpose(h1[x])
        h2_t[x] = jnp.transpose(h2[x])
        return carry

    lax.fori_loop(0, NX, turn_part, 0)
    start = pl.multiple_of(own_x * RX + (own_z // 2) * (2 * RZ), 2 * RZ)
    wanted = target_ref[pl.ds(start, 2 * RZ), :].astype(F32)
    odd = lax.rem(own_z, 2).astype(F32)
    wanted = wanted[:RZ] * (1.0 - odd) + wanted[RZ:] * odd
    wait_z(lambda z: pieces.at[z], pieces_z, sem_piece)
    rendered = jnp.sum(pieces_z[...].astype(F32), 0)
    grad_z[own_z] = (rendered - wanted).astype(BF16)
    spread_z(lambda z: grad_z.at[own_z], grad_z, sem_grad_z)
    wait_x(lambda x: trans_send.at[x], trans_all, sem_trans)

    def coef_part(x, carry):
        enc_t[x] = jnp.transpose(enc[x])
        columns = jnp.transpose(trans_all[x] * weight_rows[x])
        for slot in range(SLOTS):
            rows = pl.ds(slot * RX, RX)
            shade = colour[x, rows, :]
            coef[x, rows, :] = columns[:, slot : slot + 1] * (shade * (1.0 - shade))
        return carry

    lax.fori_loop(0, NX, coef_part, 0)
    wait_z(lambda z: grad_z.at[own_z], grad_z, sem_grad_z)
    grad_float = grad_z[...].astype(F32).reshape(RX, FEAT)
    grad_all[own_x] = grad_float.astype(BF16)
    spread_x(lambda x: grad_all.at[own_x], grad_all, sem_grad)
    grid = jnp.zeros((RX, RX), F32)
    for x in range(NX):
        dots = jnp.sum(grad_float * partial_x[x].astype(F32), -1, keepdims=True)
        grid = jnp.where(lane == x, dots, grid)
    grid = jnp.transpose(grid)
    region_own = region_z.at[own_z]
    for x in range(NX):
        region_own[x] = grid[x : x + 1] * trans_send[x]
    spread_z(lambda z: region_own, region_z, sem_region)

    def feat_part(index, carry):
        x = along_x(index)

        @pl.when(index > 0)
        def _():
            wait_x(lambda x: grad_all.at[own_x], grad_all, sem_grad, (NX - index,))

        grads = grad_all[x].astype(F32)
        grid = jnp.zeros((RX, RX), F32)
        added = jnp.zeros((8, FEAT), F32)
        for slot in range(SLOTS):
            rows = pl.ds(slot * RX, RX)
            shade = colour[x, rows, :]
            grid = jnp.where(lane == slot, jnp.sum(shade * grads, -1, keepdims=True), grid)
            found = (coef[x, rows, :] * grads).astype(BF16)
            cgrad[rows, :] = found
            added = added + to_row_groups(found.astype(F32))
        sample_rows[x] = jnp.transpose(grid)[:SLOTS]
        sum_feat[...] += added
        g_feat[...] += jnp.dot(h2_t[x], cgrad[...], preferred_element_type=F32)
        hgrad[x] = dot_nt(cgrad[...], w_feat[...])
        return carry

    lax.fori_loop(0, NX, feat_part, 0)
    feat_send[...] = g_feat[...].astype(BF16).reshape(NR, 32, FEAT)
    spread_rays(0, feat_send, feat_got)
    wait_z(lambda z: region_own, region_z, sem_region)
    below, above = x_sums(*z_sums(region_z, own_z))
    for x in range(NX):
        after_send[x] = jnp.where(onward, above[x], below[x])
    after_out[own_x] = after_send[own_x]
    spread_x(lambda x: after_send.at[x], after_out, sem_after)
    wait_x(lambda x: after_send.at[x], after_out, sem_after)

    def mid_part(x, carry):
        samples = sample_rows[x]
        later = sum_after(weight_rows[x] * samples)
        optical_grad = (
            trans_all[x] * (jnp.exp(-(before_rows[x] + optical_rows[x])) * samples - later)
            - after_out[x]
        )
        dense_grad = (
            (optical_grad * span_rows[x] * jax.nn.sigmoid(raw_rows[x])).astype(BF16).astype(F32)
        )
        columns = jnp.transpose(dense_grad)
        dense_row = vec_row[:, 2 * HID : 3 * HID]
        added = jnp.zeros((8, HID), F32)
        dense_added = jnp.zeros((8, HID), F32)
        for slot in range(SLOTS):
            rows = pl.ds(slot * RX, RX)
            hidden = h2[x, rows, :].astype(F32)
            scale = columns[:, slot : slot + 1]
            found = jnp.where(hidden > 0.0, hgrad[x, rows, :] + scale * dense_row, 0.0)
            found = found.astype(BF16)
            second[x, rows, :] = found
            added = added + to_row_groups(found.astype(F32))
            dense_added = dense_added + to_row_groups(scale * hidden)
        sum_two[...] += added
        sum_dense[...] += dense_added
        g_mid[...] += jnp.dot(h1_t[x], second[x], preferred_element_type=F32)
        return carry

    lax.fori_loop(0, NX, mid_part, 0)
    mid_send[...] = g_mid[...].astype(BF16).reshape(NR, 32, HID)
    spread_rays(1, mid_send, mid_got)

    def in_part(x, carry):
        found = jnp.where(
            h1[x].astype(F32) > 0.0, dot_nt(second[x], w_mid[...]), 0.0
        ).astype(BF16)
        first[...] = found
        sum_one[...] += to_row_groups(found.astype(F32))
        g_in[...] += jnp.dot(enc_t[x], first[...], preferred_element_type=F32)
        return carry

    lax.fori_loop(0, NX, in_part, 0)
    in_send[...] = g_in[...].astype(BF16).reshape(NR, 16, HID)
    spread_rays(2, in_send, in_got)
    sums = [
        jnp.sum(part[...], 0, keepdims=True) for part in (sum_one, sum_two, sum_dense, sum_feat)
    ]
    row = jnp.concatenate(sums + [jnp.zeros((1, 128), F32)], 1)
    for index in range(NR):
        turned = pltpu.roll(row, 1280 - PART * index, 1) if index else row
        vec_send[index] = turned[:, :WIDE]
    spread_rays(3, vec_send, vec_got)

    def own_rows(total, count):
        return total[pl.ds(pl.multiple_of(me * count, count), count), :]

    feat_out[...] = gather_rays(0, feat_send, feat_got, own_rows(g_feat, 32))
    mid_out[...] = gather_rays(1, mid_send, mid_got, own_rows(g_mid, 32))
    in_out[...] = gather_rays(2, in_send, in_got, own_rows(g_in, 16))
    vec_out[...] = gather_rays(3, vec_send, vec_got, vec_send[me])


def run_step(*operands):
    def pair(count):
        return pltpu.SemaphoreType.DMA((2, count))

    outs = (((16, 256), F32), ((32, 256), F32), ((32, 384), F32), ((1, WIDE), F32))
    outs += (((NX, 1, RX), F32),)
    scratch = (
        ((NX, ROWS, IN), BF16),
        ((NX, ROWS, HID), BF16),
        ((NX, ROWS, HID), BF16),
        ((NX, IN, ROWS), BF16),
        ((NX, HID, ROWS), BF16),
        ((NX, HID, ROWS), BF16),
        ((NX, ROWS, FEAT), F32),
        ((NX, ROWS, FEAT), F32),
        ((ROWS, FEAT), BF16),
        ((NX, ROWS, HID), F32),
        ((NX, ROWS, HID), BF16),
        ((ROWS, HID), BF16),
        ((NX, SLOTS, RX), F32),
        ((NX, SLOTS, RX), F32),
        ((NX, SLOTS, RX), F32),
        ((NX, SLOTS, RX), F32),
        ((NX, SLOTS, RX), F32),
        ((NX, SLOTS, RX), F32),
        ((HID, RX), BF16),
        ((1, 1280), F32),
        ((IN, HID), F32),
        ((HID, HID), F32),
        ((HID, FEAT), F32),
        ((8, HID), F32),
        ((8, HID), F32),
        ((8, HID), F32),
        ((8, FEAT), F32),
        ((NZ, NX, 1, RX), F32),
        ((NX, 3, 1, RX), F32),
        ((NX, 3, 1, RX), F32),
        ((NX, RX, FEAT), BF16),
        ((NX, RX, FEAT), BF16),
        ((NX, 1, RX), F32),
        ((NX, 1, RX), F32),
        ((NZ, RZ, FEAT), BF16),
        ((NZ, RZ, FEAT), BF16),
        ((NZ, RZ, FEAT), BF16),
        ((NX, RX, FEAT), BF16),
        ((NZ, NX, 1, RX), F32),
        ((NX, 1, RX), F32),
        ((NR, 16, 256), BF16),
        ((NR, 32, 256), BF16),
        ((NR, 32, 384), BF16),
        ((NR, 1, WIDE), F32),
        ((NR, 16, 256), BF16),
        ((NR, 32, 256), BF16),
        ((NR, 32, 384), BF16),
        ((NR, 1, WIDE), F32),
    )
    return pl.pallas_call(
        step_kernel,
        out_shape=tuple(jax.ShapeDtypeStruct(*out) for out in outs),
        in_specs=vmem(len(operands)),
        out_specs=tuple(vmem(len(outs))),
        scratch_shapes=[pltpu.VMEM(*part) for part in scratch]
        + [pair(NZ), pair(NX), pair(NX), pair(NX), pair(NZ), pair(NZ), pair(NX), pair(NZ), pair(NX)]
        + [pltpu.SemaphoreType.DMA((2, 4, NR))],
        compiler_params=pltpu.CompilerParams(
            collective_id=1, has_side_effects=True, vmem_limit_bytes=56 * 2**20
        ),
        name="run_step",
    )(*operands)


def adam_kernel(*refs):
    states, grads, after_ref, outs, depth_out = refs[:4], refs[4:8], refs[8], refs[9:13], refs[13]
    for state, grad, out in zip(states, grads, outs):
        gradient = grad[...].reshape((1,) + grad.shape) if len(state.shape) == 4 else grad[...]
        gradient = gradient[..., : state.shape[-1]]
        first_moment = beta_one * state[1] + (1.0 - beta_one) * gradient
        second = beta_two * state[2] + (1.0 - beta_two) * gradient * gradient
        update_step = first_moment / first_fix / (jnp.sqrt(second / second_fix) + epsilon)
        out[0] = state[0] - learn_rate * update_step
        out[1] = first_moment
        out[2] = second
    depth_out[...] = -after_ref[...]


def adam_all(states, grads, after):
    shapes = [jax.ShapeDtypeStruct(state.shape, F32) for state in states]
    shapes.append(jax.ShapeDtypeStruct(after.shape, F32))
    return pl.pallas_call(
        adam_kernel,
        out_shape=tuple(shapes),
        in_specs=vmem(9),
        out_specs=tuple(vmem(5)),
        name="adam_all",
    )(*states, *grads, after)


def per_device(
    ray_codes,
    target,
    direction,
    entries,
    exits,
    depth_bins,
    in_layer,
    mid_layer,
    feat_layer,
    vectors,
):
    in_all, mid_all, feat_all, vec_all = gather_weights(in_layer, mid_layer, feat_layer, vectors)
    *grads, after = run_step(
        ray_codes,
        depth_bins[0],
        entries,
        exits,
        direction.reshape(NX, 1, RX),
        target,
        in_all.reshape(IN, HID),
        mid_all.reshape(HID, HID),
        feat_all.reshape(HID, FEAT),
        vec_all,
    )
    *states, depth_grad = adam_all((in_layer, mid_layer, feat_layer, vectors), grads, after)
    return (*states, depth_grad.reshape(1, NX * RX))


def solution(mesh):
    placed = (
        P(None, "rays", None),
        P("rays", None),
        P("rays"),
        P("region", "rays"),
        P("region", "rays"),
        P("region", None, "rays"),
        P(None, "region", "rays", None),
        P(None, "region", "rays", None),
        P(None, "region", "rays", None),
        P(None, "region", "rays"),
    )
    return jax.shard_map(
        per_device,
        mesh=mesh,
        in_specs=placed,
        out_specs=(
            P(None, "region", "rays", None),
            P(None, "region", "rays", None),
            P(None, "region", "rays", None),
            P(None, "region", "rays"),
            P("region", "rays"),
        ),
        check_vma=False,
    )
```

time: 706 us -> 79.6 us (0.11)
  waiting for transfers between devices: 346 us -> 0 us
  blocking collectives: 282 us -> 0 us
  Pallas kernels: 0 us -> 78.7 us
  other arithmetic: 23.3 us -> 0 us
  matrix products: 18 us -> 0 us
  between operations: 15.6 us -> 0.65 us
  local copies, waits for them, and re-layouts: 10.3 us -> 0 us
  loops' own time: 8.82 us -> 0 us
    psum x1 -> x0, waiting for transfers between devices: 254 us -> none  [per_device(): rendered = lax.psum(contribution, 'region')]
    all_gather x5 -> x0, blocking collectives: 215 us -> none  [the longest x2 150 us: entering(): pieces = lax.all_gather(value, axis)]
    reduce_scatter x3 -> x0, waiting for transfers between devices: 91.7 us -> none  [the longest x1 38.9 us: per_device(): lax.psum_scatter(mid_grad, 'rays', scatter_dimension=0, tiled=True)]
    pallas_call x0 -> x3, Pallas kernels: none -> 78.7 us  [the longest x1 59.8 us: run_step(): pl.pallas_call(step_kernel, out_shape=tuple((jax.ShapeDtypeStruct(*out) f...]
    unnamed x2 -> x0, blocking collectives: 67.5 us -> none
    dot_general x10 -> x0, matrix products: 18 us -> none  [the longest x1 3.96 us: backward(): jnp.dot(hidden_two.T, colour_grad, preferred_element_type=jnp.float32)]
    another operation x4 -> x0, loops' own time: 8.82 us -> none  [entering(): return lax.fori_loop(0, count - 1, lap, total)]
    reduce_sum x4 -> x0, other arithmetic: 7.79 us -> none  [the longest x1 5.09 us: backward(): jnp.sum(colour_grad, 0, dtype=jnp.float32)]
  transfers between devices with their start and end apart: 4 -> 0, of which waited for: 4 -> 0; matrix products, arithmetic and copies ran while one was open for 1% -> 0% of each run, Pallas kernels for 0% -> 0%
where the time goes in v2:
time: 79.6 us; the launch traced here: 79.3 us
  Pallas kernels  78.7 us (99%)
    pallas_call x1, Pallas kernels, run_step(): pl.pallas_call(step_kernel, out_shape=tuple((jax.ShapeDtypeStruct(*out) f...  59.8 us
    pallas_call x1, Pallas kernels, gather_weights(): pl.pallas_call(gather_kernel, out_shape=shapes, in_specs=[pl.BlockSpec(me...  17.1 us
    pallas_call x1, Pallas kernels, adam_all(): pl.pallas_call(adam_kernel, out_shape=tuple(shapes), in_specs=vmem(9), ou...  1.79 us

profile of v2, /device:TPU:1, one launch (start us, length us, event | category | flops | bytes accessed | tf_op | source)
XLA Modules:
  0.0 79.3 jit_solution(2049588888014461662)
XLA Ops:
  0.6 17.1 %gather_weights.1 = (bf16[8,16,256]{2,1,0:T(8,128)(2,1)}, bf16[8,32,256]{2,1,0:T(8,128)(2,1)}, bf16[8,32,384]{2,1,0:T(8,128)(2,1)}, f32[8,1,256]{2,1,0:T(1,128)}) custom-call(f32[3,1,16,256]{3,2,1,0:T(8,128)} %refs_0_.1, f32[3,1,32,256]{3,2,1,0:T(8,128)} %refs_1_.1, f32[3,1,32,384]{3,2,1,0:T(8,128)} %refs_2_.1, f32[3,1,144]{2,1,0:T(1,128)} %refs_3_.1), custom_call_target="tpu_custom_call" | custom-call | tf_op jit(solution)/shard_map/gather_weights/pallas_call | solution.py:120
  17.7 59.8 %run_step.1 = (f32[16,256]{1,0:T(8,128)}, f32[32,256]{1,0:T(8,128)}, f32[32,384]{1,0:T(8,128)}, f32[1,256]{1,0:T(1,128)}, f32[4,1,128]{2,1,0:T(1,128)}) custom-call(bf16[2,512,128]{2,1,0:T(8,128)(2,1)} %codes_ref.1, s32[8,512]{1,0:T(8,128)} %bitcast.9, s32[1,512]{1,0:T(1,128)} %entry_ref.1, s32[1,512]{1,0:T(1,128)} %exit_ref.1, s32[4,1,128]{2,1,0:T(1,128)} %bitcast.10, ...), custom_call_target="tpu_custom_call" | custom-call | tf_op jit(solution)/shard_map/run_step/pallas_call | solution.py:659
  77.6 1.8 %adam_all.1 = (f32[3,1,16,256]{3,2,1,0:T(8,128)}, f32[3,1,32,256]{3,2,1,0:T(8,128)}, f32[3,1,32,384]{3,2,1,0:T(8,128)}, f32[3,1,144]{2,1,0:T(1,128)}, f32[4,1,128]{2,1,0:T(1,128)}) custom-call(f32[3,1,16,256]{3,2,1,0:T(8,128)} %refs_0_.1, f32[3,1,32,256]{3,2,1,0:T(8,128)} %refs_1_.1, f32[3,1,32,384]{3,2,1,0:T(8,128)} %refs_2_.1, f32[3,1,144]{2,1,0:T(1,128)} %refs_3_.1, ...), custom_call_target="tpu_custom_call" | custom-call | tf_op jit(solution)/shard_map/adam_all/pallas_call | solution.py:691

commit v3 on v2

--- a/solution.py
+++ b/solution.py
@@ -48,94 +48,6 @@
     )
 
 
-def gather_kernel(
-    in_ref,
-    mid_ref,
-    feat_ref,
-    vec_ref,
-    in_out,
-    mid_out,
-    feat_out,
-    vec_out,
-    in_own,
-    mid_own,
-    feat_own,
-    vec_own,
-    load_sem,
-    send_sem,
-    recv_sem,
-):
-    me = lax.axis_index("rays")
-    barrier = pltpu.get_barrier_semaphore()
-    for step in range(1, NR):
-        pl.semaphore_signal(
-            barrier, inc=1, device_id={"rays": lax.rem(me + step, NR)}, device_id_type=MESH
-        )
-    loads = (
-        pltpu.make_async_copy(in_ref.at[0, 0], in_own, load_sem.at[0]),
-        pltpu.make_async_copy(mid_ref.at[0, 0], mid_own, load_sem.at[1]),
-        pltpu.make_async_copy(feat_ref.at[0, 0], feat_own, load_sem.at[2]),
-        pltpu.make_async_copy(vec_ref.at[0], vec_own, load_sem.at[3]),
-    )
-    for load in loads:
-        load.start()
-    for load in loads:
-        load.wait()
-    in_out[me] = in_own[...].astype(BF16)
-    mid_out[me] = mid_own[...].astype(BF16)
-    feat_out[me] = feat_own[...].astype(BF16)
-    vec_out[me] = jnp.zeros((1, WIDE), F32)
-    vec_out[me, :, pl.ds(0, PART)] = vec_own[...].astype(BF16).astype(F32)
-    pl.semaphore_wait(barrier, NR - 1)
-    outs = (in_out, mid_out, vec_out, feat_out)
-    for kind, out in enumerate(outs):
-        for step in range(1, NR):
-            peer = lax.rem(me + step, NR)
-            remote(
-                out.at[me],
-                out.at[me],
-                send_sem.at[kind, step],
-                recv_sem.at[kind, step],
-                {"rays": peer},
-            ).start()
-    for kind, out in enumerate(outs):
-        for step in range(1, NR):
-            origin = lax.rem(me + NR - step, NR)
-            remote(
-                out.at[origin],
-                out.at[origin],
-                send_sem.at[kind, step],
-                recv_sem.at[kind, step],
-                {"rays": origin},
-            ).wait()
-
-
-def gather_weights(in_layer, mid_layer, feat_layer, vectors):
-    shapes = (
-        jax.ShapeDtypeStruct((NR, 16, 256), BF16),
-        jax.ShapeDtypeStruct((NR, 32, 256), BF16),
-        jax.ShapeDtypeStruct((NR, 32, 384), BF16),
-        jax.ShapeDtypeStruct((NR, 1, WIDE), F32),
-    )
-    return pl.pallas_call(
-        gather_kernel,
-        out_shape=shapes,
-        in_specs=[pl.BlockSpec(memory_space=pl.ANY)] * 4,
-        out_specs=tuple(vmem(4)),
-        scratch_shapes=[
-            pltpu.VMEM((16, 256), F32),
-            pltpu.VMEM((32, 256), F32),
-            pltpu.VMEM((32, 384), F32),
-            pltpu.VMEM((1, PART), F32),
-            pltpu.SemaphoreType.DMA((4,)),
-            pltpu.SemaphoreType.DMA((4, NR)),
-            pltpu.SemaphoreType.DMA((4, NR)),
-        ],
-        compiler_params=pltpu.CompilerParams(collective_id=0, has_side_effects=True),
-        name="gather_weights",
-    )(in_layer, mid_layer, feat_layer, vectors)
-
-
 def far_first(count):
     half = count // 2
     order = [half]
@@ -204,21 +116,35 @@
 
 
 def step_kernel(
+    codes_hbm,
+    bins_hbm,
+    entry_hbm,
+    exit_hbm,
+    onward_hbm,
+    target_hbm,
+    in_layer,
+    mid_layer,
+    feat_layer,
+    vectors,
+    in_out,
+    mid_out,
+    feat_out,
+    vec_out,
+    after_out,
     codes_ref,
     bins_ref,
     entry_ref,
     exit_ref,
     onward_ref,
     target_ref,
+    in_own,
+    mid_own,
+    feat_own,
+    vec_own,
     w_in,
     w_mid,
     w_feat,
     vec_ref,
-    in_out,
-    mid_out,
-    feat_out,
-    vec_out,
-    after_out,
     enc,
     h1,
     h2,
@@ -277,6 +203,8 @@
     sem_region,
     sem_after,
     sem_rays,
+    sem_load,
+    sem_weight,
 ):
     place = lax.axis_index("region")
     me = lax.axis_index("rays")
@@ -356,10 +284,99 @@
             total = total + target[step].astype(F32)
         return total
 
+    loads = [
+        pltpu.make_async_copy(source, target, sem_load.at[index])
+        for index, (source, target) in enumerate(
+            (
+                (in_layer.at[0, 0], in_own),
+                (mid_layer.at[0, 0], mid_own),
+                (feat_layer.at[0, 0], feat_own),
+                (vectors.at[0], vec_own),
+                (codes_hbm, codes_ref),
+                (bins_hbm.at[0], bins_ref),
+                (entry_hbm, entry_ref),
+                (exit_hbm, exit_ref),
+                (onward_hbm, onward_ref),
+                (target_hbm, target_ref),
+            )
+        )
+    ]
+    for load in loads:
+        load.start()
+
+    def mine(array, count, index):
+        return array.at[pl.ds(pl.multiple_of(index * count, count), count)]
+
+    weights = (
+        lambda index: mine(w_in, 16, index),
+        lambda index: mine(w_mid, 32, index),
+        lambda index: vec_ref.at[index],
+        lambda index: mine(w_feat, 32, index),
+    )
+
+    def spread_weights(kind):
+        for step in range(1, NR):
+            remote(
+                weights[kind](me),
+                weights[kind](me),
+                sem_weight.at[0, kind, step],
+                sem_weight.at[1, kind, step],
+                {"rays": lax.rem(me + step, NR)},
+            ).start()
+
+    def wait_weights(kind):
+        for step in range(1, NR):
+            origin = lax.rem(me + NR - step, NR)
+            remote(
+                weights[kind](origin),
+                weights[kind](origin),
+                sem_weight.at[0, kind, step],
+                sem_weight.at[1, kind, step],
+                {"rays": origin},
+            ).wait()
+
     unit = depth_scale / (NX * NZ * BINS)
     lane = lax.broadcasted_iota(jnp.int32, (RX, RX), 1)
     slot_row = lax.broadcasted_iota(jnp.int32, (SLOTS, RX), 0)
-
+    for load in loads[:4]:
+        load.wait()
+    weights[0](me)[...] = in_own[...].astype(BF16)
+    weights[1](me)[...] = mid_own[...].astype(BF16)
+    weights[3](me)[...] = feat_own[...].astype(BF16)
+    vec_ref[me] = jnp.zeros((1, WIDE), F32)
+    vec_ref[me, :, pl.ds(0, PART)] = vec_own[...].astype(BF16).astype(F32)
+    for load in loads[4:]:
+        load.wait()
+    for total in (g_in, g_mid, g_feat, sum_one, sum_two, sum_dense, sum_feat):
+        total[...] = jnp.zeros(total.shape, F32)
+
+    def code_part(x, carry):
+        lanes = pl.ds(pl.multiple_of(x * RX, RX), RX)
+        bins = bins_ref[:, lanes].astype(F32)
+        columns = jnp.transpose((bins + 0.5) / BINS)
+        anchor = codes_ref[0, lanes, :].astype(F32)
+        heading = codes_ref[1, lanes, :].astype(F32)
+        for slot in range(SLOTS):
+            enc[x, pl.ds(slot * RX, RX), :] = (
+                anchor + columns[:, slot : slot + 1] * heading
+            ).astype(BF16)
+        following = jnp.concatenate([bins[1:], jnp.full((1, RX), float(BINS), F32)], 0)
+        inside = (slot_row >= entry_ref[:, lanes]) & (slot_row < exit_ref[:, lanes])
+        span_rows[x] = jnp.where(inside, (following - bins) * unit, 0.0)
+        return carry
+
+    lax.fori_loop(0, NX, code_part, 0)
+    pl.semaphore_wait(barrier, NX + NZ + NR - 3)
+    for kind in range(4):
+        spread_weights(kind)
+
+    def turn_code(x, carry):
+        enc_t[x] = jnp.transpose(enc[x])
+        return carry
+
+    lax.fori_loop(0, NX, turn_code, 0)
+    for kind in range(3):
+        wait_weights(kind)
     row = jnp.zeros((1, 1280), F32)
     tail = jnp.zeros((1, 1280 - WIDE), F32)
     for index in range(NR):
@@ -369,22 +386,11 @@
     dense_wide[...] = jnp.transpose(
         jnp.broadcast_to(row[:, 2 * HID : 3 * HID], (RX, HID))
     ).astype(BF16)
-    for total in (g_in, g_mid, g_feat, sum_one, sum_two, sum_dense, sum_feat):
-        total[...] = jnp.zeros(total.shape, F32)
 
     depth_own = depth_z.at[own_z]
 
     def hidden_part(index, carry):
         x = along_x(index + 1)
-        lanes = pl.ds(pl.multiple_of(x * RX, RX), RX)
-        bins = bins_ref[:, lanes].astype(F32)
-        columns = jnp.transpose((bins + 0.5) / BINS)
-        anchor = codes_ref[0, lanes, :].astype(F32)
-        heading = codes_ref[1, lanes, :].astype(F32)
-        for slot in range(SLOTS):
-            enc[x, pl.ds(slot * RX, RX), :] = (
-                anchor + columns[:, slot : slot + 1] * heading
-            ).astype(BF16)
         h1[x] = jnp.maximum(
             jnp.dot(enc[x], w_in[...], preferred_element_type=F32) + vec_row[:, :HID], 0.0
         ).astype(BF16)
@@ -397,23 +403,19 @@
         for slot in range(SLOTS):
             grid = jnp.where(lane == slot, dense[slot * RX : (slot + 1) * RX], grid)
         raw = jnp.transpose(grid)[:SLOTS]
-        following = jnp.concatenate([bins[1:], jnp.full((1, RX), float(BINS), F32)], 0)
-        inside = (slot_row >= entry_ref[:, lanes]) & (slot_row < exit_ref[:, lanes])
-        span = jnp.where(inside, (following - bins) * unit, 0.0)
         soft = jnp.maximum(raw, 0.0) + jnp.log1p(jnp.exp(-jnp.abs(raw)))
-        optical = soft * span
+        optical = soft * span_rows[x]
         before, total = sum_before(optical)
         raw_rows[x] = raw
         optical_rows[x] = optical
         before_rows[x] = before
         weight_rows[x] = jnp.exp(-before) * one_less_exp(optical)
-        span_rows[x] = span
         depth_own[x] = total
         return carry
 
     lax.fori_loop(0, NX, hidden_part, 0)
-    pl.semaphore_wait(barrier, NX + NZ + NR - 3)
     spread_z(lambda z: depth_own, depth_z, sem_depth)
+    wait_weights(3)
 
     def colour_part(index, carry):
         x = along_x(index + 1)
@@ -481,7 +483,6 @@
     wait_x(lambda x: trans_send.at[x], trans_all, sem_trans)
 
     def coef_part(x, carry):
-        enc_t[x] = jnp.transpose(enc[x])
         columns = jnp.transpose(trans_all[x] * weight_rows[x])
         for slot in range(SLOTS):
             rows = pl.ds(slot * RX, RX)
@@ -607,6 +608,20 @@
     outs = (((16, 256), F32), ((32, 256), F32), ((32, 384), F32), ((1, WIDE), F32))
     outs += (((NX, 1, RX), F32),)
     scratch = (
+        ((2, NX * RX, IN), BF16),
+        ((SLOTS, NX * RX), jnp.int32),
+        ((1, NX * RX), jnp.int32),
+        ((1, NX * RX), jnp.int32),
+        ((NX, 1, RX), jnp.int32),
+        ((NX * RX, FEAT), BF16),
+        ((16, HID), F32),
+        ((32, HID), F32),
+        ((32, FEAT), F32),
+        ((1, PART), F32),
+        ((IN, HID), BF16),
+        ((HID, HID), BF16),
+        ((HID, FEAT), BF16),
+        ((NR, 1, WIDE), F32),
         ((NX, ROWS, IN), BF16),
         ((NX, ROWS, HID), BF16),
         ((NX, ROWS, HID), BF16),
@@ -659,13 +674,14 @@
     return pl.pallas_call(
         step_kernel,
         out_shape=tuple(jax.ShapeDtypeStruct(*out) for out in outs),
-        in_specs=vmem(len(operands)),
+        in_specs=[pl.BlockSpec(memory_space=pl.ANY)] * len(operands),
         out_specs=tuple(vmem(len(outs))),
         scratch_shapes=[pltpu.VMEM(*part) for part in scratch]
         + [pair(NZ), pair(NX), pair(NX), pair(NX), pair(NZ), pair(NZ), pair(NX), pair(NZ), pair(NX)]
+        + [pltpu.SemaphoreType.DMA((2, 4, NR)), pltpu.SemaphoreType.DMA((10,))]
         + [pltpu.SemaphoreType.DMA((2, 4, NR))],
         compiler_params=pltpu.CompilerParams(
-            collective_id=1, has_side_effects=True, vmem_limit_bytes=56 * 2**20
+            collective_id=0, has_side_effects=True, vmem_limit_bytes=60 * 2**20
         ),
         name="run_step",
     )(*operands)
@@ -709,18 +725,17 @@
     feat_layer,
     vectors,
 ):
-    in_all, mid_all, feat_all, vec_all = gather_weights(in_layer, mid_layer, feat_layer, vectors)
     *grads, after = run_step(
         ray_codes,
-        depth_bins[0],
+        depth_bins,
         entries,
         exits,
         direction.reshape(NX, 1, RX),
         target,
-        in_all.reshape(IN, HID),
-        mid_all.reshape(HID, HID),
-        feat_all.reshape(HID, FEAT),
-        vec_all,
+        in_layer,
+        mid_layer,
+        feat_layer,
+        vectors,
     )
     *states, depth_grad = adam_all((in_layer, mid_layer, feat_layer, vectors), grads, after)
     return (*states, depth_grad.reshape(1, NX * RX))

time: 79.6 us -> 76.8 us (0.965)
  Pallas kernels: 78.7 us -> 76 us
    pallas_call x1 -> x0, Pallas kernels: 17.1 us -> none  [gather_weights(): pl.pallas_call(gather_kernel, out_shape=shapes, in_specs=[pl.BlockSpec(me...]
    pallas_call x1, Pallas kernels: 59.8 us -> 74.2 us  [run_step(): pl.pallas_call(step_kernel, out_shape=tuple((jax.ShapeDtypeStruct(*out) f...]
where the time goes in v3:
time: 76.8 us; the launch traced here: 76.6 us
  Pallas kernels  76 us (99%)
    pallas_call x1, Pallas kernels, run_step(): pl.pallas_call(step_kernel, out_shape=tuple((jax.ShapeDtypeStruct(*out) f...  74.2 us
    pallas_call x1, Pallas kernels, adam_all(): pl.pallas_call(adam_kernel, out_shape=tuple(shapes), in_specs=vmem(9), ou...  1.79 us

profile of v3, /device:TPU:1, one launch (start us, length us, event | category | flops | bytes accessed | tf_op | source)
XLA Modules:
  0.0 76.6 jit_solution(4606686757700273935)
XLA Ops:
  0.6 74.2 %run_step.1 = (f32[16,256]{1,0:T(8,128)}, f32[32,256]{1,0:T(8,128)}, f32[32,384]{1,0:T(8,128)}, f32[1,256]{1,0:T(1,128)}, f32[4,1,128]{2,1,0:T(1,128)}) custom-call(bf16[2,512,128]{2,1,0:T(8,128)(2,1)} %codes_hbm.1, s32[1,8,512]{2,1,0:T(8,128)} %bins_hbm.1, s32[1,512]{1,0:T(1,128)} %entry_hbm.1, s32[1,512]{1,0:T(1,128)} %exit_hbm.1, s32[4,1,128]{2,1,0:T(1,128)} %bitcast.2, ...), custom_call_target="tpu_custom_call" | custom-call | tf_op jit(solution)/shard_map/run_step/pallas_call | solution.py:674
  74.8 1.8 %adam_all.1 = (f32[3,1,16,256]{3,2,1,0:T(8,128)}, f32[3,1,32,256]{3,2,1,0:T(8,128)}, f32[3,1,32,384]{3,2,1,0:T(8,128)}, f32[3,1,144]{2,1,0:T(1,128)}, f32[4,1,128]{2,1,0:T(1,128)}) custom-call(f32[3,1,16,256]{3,2,1,0:T(8,128)} %refs_0_.1, f32[3,1,32,256]{3,2,1,0:T(8,128)} %refs_1_.1, f32[3,1,32,384]{3,2,1,0:T(8,128)} %refs_2_.1, f32[3,1,144]{2,1,0:T(1,128)} %refs_3_.1, ...), custom_call_target="tpu_custom_call" | custom-call | tf_op jit(solution)/shard_map/adam_all/pallas_call | solution.py:707

commit v4 on v3

--- a/solution.py
+++ b/solution.py
@@ -61,11 +61,18 @@
     lower = jnp.zeros((NX, 1, RX), F32)
     upper = jnp.zeros((NX, 1, RX), F32)
     for z in range(NZ):
-        rows = table[z]
+        rows = table[:, z]
         column = column + rows
         lower = lower + rows * (z < own_z).astype(F32)
         upper = upper + rows * (z > own_z).astype(F32)
     return column, lower, upper
+
+
+def far_regions():
+    hops = [
+        (min(x, NX - x) + min(z, NZ - z), x, z) for x in range(NX) for z in range(NZ) if x + z
+    ]
+    return [(x, z) for _, x, z in sorted(hops, reverse=True)]
 
 
 def x_sums(column, lower, upper):
@@ -90,21 +97,21 @@
 
 
 def sum_before(rows):
-    running = jnp.zeros((1, RX), F32)
+    running = jnp.zeros((NX, 1, RX), F32)
     found = []
     for slot in range(SLOTS):
         found.append(running)
-        running = running + rows[slot : slot + 1]
-    return jnp.concatenate(found, 0), running
+        running = running + rows[:, slot : slot + 1]
+    return jnp.concatenate(found, 1), running
 
 
 def sum_after(rows):
-    running = jnp.zeros((1, RX), F32)
+    running = jnp.zeros((NX, 1, RX), F32)
     found = []
     for slot in range(SLOTS - 1, -1, -1):
         found.append(running)
-        running = running + rows[slot : slot + 1]
-    return jnp.concatenate(found[::-1], 0)
+        running = running + rows[:, slot : slot + 1]
+    return jnp.concatenate(found[::-1], 1)
 
 
 def to_row_groups(values):
@@ -168,13 +175,10 @@
     g_in,
     g_mid,
     g_feat,
-    sum_one,
-    sum_two,
     sum_dense,
-    sum_feat,
-    depth_z,
-    stats_send,
-    stats_x,
+    dense_columns,
+    depth_send,
+    depth_all,
     partial_send,
     partial_x,
     trans_send,
@@ -183,8 +187,8 @@
     pieces_z,
     grad_z,
     grad_all,
-    region_z,
-    after_send,
+    region_send,
+    region_all,
     in_send,
     mid_send,
     feat_send,
@@ -194,14 +198,12 @@
     feat_got,
     vec_got,
     sem_depth,
-    sem_stats,
     sem_partial,
     sem_trans,
     sem_piece,
     sem_grad_z,
     sem_grad,
     sem_region,
-    sem_after,
     sem_rays,
     sem_load,
     sem_weight,
@@ -220,13 +222,9 @@
         return {"region": x * NZ + z}
 
     barrier = pltpu.get_barrier_semaphore()
-    for step in range(1, NZ):
+    for far_x, far_z in far_regions():
         pl.semaphore_signal(
-            barrier, inc=1, device_id=at(own_x, along_z(step)), device_id_type=MESH
-        )
-    for step in range(1, NX):
-        pl.semaphore_signal(
-            barrier, inc=1, device_id=at(along_x(step), own_z), device_id_type=MESH
+            barrier, inc=1, device_id=at(along_x(far_x), along_z(far_z)), device_id_type=MESH
         )
     for step in range(1, NR):
         pl.semaphore_signal(
@@ -259,6 +257,22 @@
         for step in far_first(NZ)[::-1]:
             z = along_z(NZ - step)
             remote(source(z), target.at[z], sems.at[0, step], sems.at[1, step], at(own_x, z)).wait()
+
+    def spread_all(source, target, sems):
+        for far_x, far_z in far_regions():
+            x, z = along_x(far_x), along_z(far_z)
+            index = far_x * NZ + far_z
+            remote(
+                source(x), target.at[own_x, own_z], sems.at[0, index], sems.at[1, index], at(x, z)
+            ).start()
+
+    def wait_all(source, target, sems):
+        for far_x, far_z in far_regions()[::-1]:
+            x, z = along_x(NX - far_x), along_z(NZ - far_z)
+            index = far_x * NZ + far_z
+            remote(
+                source(x), target.at[x, z], sems.at[0, index], sems.at[1, index], at(x, z)
+            ).wait()
 
     def spread_rays(kind, source, target):
         for step in range(1, NR):
@@ -347,8 +361,13 @@
     vec_ref[me, :, pl.ds(0, PART)] = vec_own[...].astype(BF16).astype(F32)
     for load in loads[4:]:
         load.wait()
-    for total in (g_in, g_mid, g_feat, sum_one, sum_two, sum_dense, sum_feat):
+    for total in (g_in, g_mid, g_feat, sum_dense):
         total[...] = jnp.zeros(total.shape, F32)
+    ones = jnp.ones((16, ROWS), BF16)
+    for x in range(NX):
+        enc_t[x, pl.ds(IN, 16), :] = ones
+        h1_t[x, pl.ds(HID, 16), :] = ones
+        h2_t[x, pl.ds(HID, 16), :] = ones
 
     def code_part(x, carry):
         lanes = pl.ds(pl.multiple_of(x * RX, RX), RX)
@@ -366,12 +385,12 @@
         return carry
 
     lax.fori_loop(0, NX, code_part, 0)
-    pl.semaphore_wait(barrier, NX + NZ + NR - 3)
+    pl.semaphore_wait(barrier, NX * NZ + NR - 2)
     for kind in range(4):
         spread_weights(kind)
 
     def turn_code(x, carry):
-        enc_t[x] = jnp.transpose(enc[x])
+        enc_t[x, pl.ds(0, IN), :] = jnp.transpose(enc[x])
         return carry
 
     lax.fori_loop(0, NX, turn_code, 0)
@@ -386,8 +405,6 @@
     dense_wide[...] = jnp.transpose(
         jnp.broadcast_to(row[:, 2 * HID : 3 * HID], (RX, HID))
     ).astype(BF16)
-
-    depth_own = depth_z.at[own_z]
 
     def hidden_part(index, carry):
         x = along_x(index + 1)
@@ -402,19 +419,20 @@
         grid = jnp.zeros((RX, RX), F32)
         for slot in range(SLOTS):
             grid = jnp.where(lane == slot, dense[slot * RX : (slot + 1) * RX], grid)
-        raw = jnp.transpose(grid)[:SLOTS]
-        soft = jnp.maximum(raw, 0.0) + jnp.log1p(jnp.exp(-jnp.abs(raw)))
-        optical = soft * span_rows[x]
-        before, total = sum_before(optical)
-        raw_rows[x] = raw
-        optical_rows[x] = optical
-        before_rows[x] = before
-        weight_rows[x] = jnp.exp(-before) * one_less_exp(optical)
-        depth_own[x] = total
+        raw_rows[x] = jnp.transpose(grid)[:SLOTS]
         return carry
 
     lax.fori_loop(0, NX, hidden_part, 0)
-    spread_z(lambda z: depth_own, depth_z, sem_depth)
+    raw = raw_rows[...]
+    soft = jnp.maximum(raw, 0.0) + jnp.log1p(jnp.exp(-jnp.abs(raw)))
+    optical = soft * span_rows[...]
+    before, total = sum_before(optical)
+    depth_send[...] = total
+    spread_all(lambda x: depth_send.at[x], depth_all, sem_depth)
+    depth_all[own_x, own_z] = depth_send[own_x]
+    optical_rows[...] = optical
+    before_rows[...] = before
+    weight_rows[...] = jnp.exp(-before) * one_less_exp(optical)
     wait_weights(3)
 
     def colour_part(index, carry):
@@ -437,20 +455,8 @@
 
     lax.fori_loop(0, NX, colour_part, 0)
     partial_x[own_x] = partial_send[own_x]
-    wait_z(lambda z: depth_own, depth_z, sem_depth)
-    column, lower, upper = z_sums(depth_z, own_z)
-    for x in range(NX):
-        stats_send[x, 0] = column[x]
-        stats_send[x, 1] = lower[x]
-        stats_send[x, 2] = upper[x]
-    stats_x[own_x] = stats_send[own_x]
-    spread_x(lambda x: stats_send.at[x], stats_x, sem_stats)
-    wait_x(lambda x: stats_send.at[x], stats_x, sem_stats)
-    below, above = x_sums(
-        [stats_x[x, 0] for x in range(NX)],
-        [stats_x[x, 1] for x in range(NX)],
-        [stats_x[x, 2] for x in range(NX)],
-    )
+    wait_all(lambda x: depth_send.at[x], depth_all, sem_depth)
+    below, above = x_sums(*z_sums(depth_all, own_z))
     onward = onward_ref[own_x] == 0
     trans = [jnp.exp(-jnp.where(onward, below[x], above[x])) for x in range(NX)]
     for x in range(NX):
@@ -467,8 +473,8 @@
     pieces_z[own_z] = pieces[own_z]
 
     def turn_part(x, carry):
-        h1_t[x] = jnp.transpose(h1[x])
-        h2_t[x] = jnp.transpose(h2[x])
+        h1_t[x, pl.ds(0, HID), :] = jnp.transpose(h1[x])
+        h2_t[x, pl.ds(0, HID), :] = jnp.transpose(h2[x])
         return carry
 
     lax.fori_loop(0, NX, turn_part, 0)
@@ -500,10 +506,10 @@
         dots = jnp.sum(grad_float * partial_x[x].astype(F32), -1, keepdims=True)
         grid = jnp.where(lane == x, dots, grid)
     grid = jnp.transpose(grid)
-    region_own = region_z.at[own_z]
     for x in range(NX):
-        region_own[x] = grid[x : x + 1] * trans_send[x]
-    spread_z(lambda z: region_own, region_z, sem_region)
+        region_send[x] = grid[x : x + 1] * trans_send[x]
+    spread_all(lambda x: region_send, region_all, sem_region)
+    region_all[own_x, own_z] = region_send[...]
 
     def feat_part(index, carry):
         x = along_x(index)
@@ -514,77 +520,73 @@
 
         grads = grad_all[x].astype(F32)
         grid = jnp.zeros((RX, RX), F32)
-        added = jnp.zeros((8, FEAT), F32)
         for slot in range(SLOTS):
             rows = pl.ds(slot * RX, RX)
             shade = colour[x, rows, :]
             grid = jnp.where(lane == slot, jnp.sum(shade * grads, -1, keepdims=True), grid)
-            found = (coef[x, rows, :] * grads).astype(BF16)
-            cgrad[rows, :] = found
-            added = added + to_row_groups(found.astype(F32))
+            cgrad[rows, :] = (coef[x, rows, :] * grads).astype(BF16)
         sample_rows[x] = jnp.transpose(grid)[:SLOTS]
-        sum_feat[...] += added
         g_feat[...] += jnp.dot(h2_t[x], cgrad[...], preferred_element_type=F32)
         hgrad[x] = dot_nt(cgrad[...], w_feat[...])
         return carry
 
     lax.fori_loop(0, NX, feat_part, 0)
-    feat_send[...] = g_feat[...].astype(BF16).reshape(NR, 32, FEAT)
+    feat_send[...] = g_feat[pl.ds(0, HID), :].astype(BF16).reshape(NR, 32, FEAT)
     spread_rays(0, feat_send, feat_got)
-    wait_z(lambda z: region_own, region_z, sem_region)
-    below, above = x_sums(*z_sums(region_z, own_z))
+    samples = sample_rows[...]
+    later = sum_after(weight_rows[...] * samples)
+    local_grad = trans_all[...] * (
+        jnp.exp(-(before_rows[...] + optical_rows[...])) * samples - later
+    )
+    dense_scale = span_rows[...] * jax.nn.sigmoid(raw_rows[...])
+    wait_all(lambda x: region_send, region_all, sem_region)
+    above = jnp.zeros((NX, 1, RX), F32)
+    below = jnp.zeros((NX, 1, RX), F32)
     for x in range(NX):
-        after_send[x] = jnp.where(onward, above[x], below[x])
-    after_out[own_x] = after_send[own_x]
-    spread_x(lambda x: after_send.at[x], after_out, sem_after)
-    wait_x(lambda x: after_send.at[x], after_out, sem_after)
+        for z in range(NZ):
+            rows = region_all[:, z, x]
+            above = above + rows * (x * NZ + z > place).astype(F32)
+            below = below + rows * (x * NZ + z < place).astype(F32)
+    after = jnp.where(onward_ref[...] == 0, above, below)
+    after_out[...] = after
+    dense_grad = ((local_grad - after) * dense_scale).astype(BF16).astype(F32)
+    for x in range(NX):
+        dense_columns[x] = jnp.transpose(dense_grad[x])
 
     def mid_part(x, carry):
-        samples = sample_rows[x]
-        later = sum_after(weight_rows[x] * samples)
-        optical_grad = (
-            trans_all[x] * (jnp.exp(-(before_rows[x] + optical_rows[x])) * samples - later)
-            - after_out[x]
-        )
-        dense_grad = (
-            (optical_grad * span_rows[x] * jax.nn.sigmoid(raw_rows[x])).astype(BF16).astype(F32)
-        )
-        columns = jnp.transpose(dense_grad)
+        columns = dense_columns[x]
         dense_row = vec_row[:, 2 * HID : 3 * HID]
-        added = jnp.zeros((8, HID), F32)
         dense_added = jnp.zeros((8, HID), F32)
         for slot in range(SLOTS):
             rows = pl.ds(slot * RX, RX)
             hidden = h2[x, rows, :].astype(F32)
             scale = columns[:, slot : slot + 1]
             found = jnp.where(hidden > 0.0, hgrad[x, rows, :] + scale * dense_row, 0.0)
-            found = found.astype(BF16)
-            second[x, rows, :] = found
-            added = added + to_row_groups(found.astype(F32))
+            second[x, rows, :] = found.astype(BF16)
             dense_added = dense_added + to_row_groups(scale * hidden)
-        sum_two[...] += added
         sum_dense[...] += dense_added
         g_mid[...] += jnp.dot(h1_t[x], second[x], preferred_element_type=F32)
         return carry
 
     lax.fori_loop(0, NX, mid_part, 0)
-    mid_send[...] = g_mid[...].astype(BF16).reshape(NR, 32, HID)
+    mid_send[...] = g_mid[pl.ds(0, HID), :].astype(BF16).reshape(NR, 32, HID)
     spread_rays(1, mid_send, mid_got)
 
     def in_part(x, carry):
-        found = jnp.where(
+        first[...] = jnp.where(
             h1[x].astype(F32) > 0.0, dot_nt(second[x], w_mid[...]), 0.0
         ).astype(BF16)
-        first[...] = found
-        sum_one[...] += to_row_groups(found.astype(F32))
         g_in[...] += jnp.dot(enc_t[x], first[...], preferred_element_type=F32)
         return carry
 
     lax.fori_loop(0, NX, in_part, 0)
-    in_send[...] = g_in[...].astype(BF16).reshape(NR, 16, HID)
+    in_send[...] = g_in[pl.ds(0, IN), :].astype(BF16).reshape(NR, 16, HID)
     spread_rays(2, in_send, in_got)
     sums = [
-        jnp.sum(part[...], 0, keepdims=True) for part in (sum_one, sum_two, sum_dense, sum_feat)
+        g_in[pl.ds(IN, 8), :][:1],
+        g_mid[pl.ds(HID, 8), :][:1],
+        jnp.sum(sum_dense[...], 0, keepdims=True),
+        g_feat[pl.ds(HID, 8), :][:1],
     ]
     row = jnp.concatenate(sums + [jnp.zeros((1, 128), F32)], 1)
     for index in range(NR):
@@ -625,9 +627,9 @@
         ((NX, ROWS, IN), BF16),
         ((NX, ROWS, HID), BF16),
         ((NX, ROWS, HID), BF16),
-        ((NX, IN, ROWS), BF16),
-        ((NX, HID, ROWS), BF16),
-        ((NX, HID, ROWS), BF16),
+        ((NX, IN + 16, ROWS), BF16),
+        ((NX, HID + 16, ROWS), BF16),
+        ((NX, HID + 16, ROWS), BF16),
         ((NX, ROWS, FEAT), F32),
         ((NX, ROWS, FEAT), F32),
         ((ROWS, FEAT), BF16),
@@ -642,16 +644,13 @@
         ((NX, SLOTS, RX), F32),
         ((HID, RX), BF16),
         ((1, 1280), F32),
-        ((IN, HID), F32),
-        ((HID, HID), F32),
-        ((HID, FEAT), F32),
+        ((IN + 16, HID), F32),
+        ((HID + 16, HID), F32),
+        ((HID + 16, FEAT), F32),
         ((8, HID), F32),
-        ((8, HID), F32),
-        ((8, HID), F32),
-        ((8, FEAT), F32),
-        ((NZ, NX, 1, RX), F32),
-        ((NX, 3, 1, RX), F32),
-        ((NX, 3, 1, RX), F32),
+        ((NX, RX, SLOTS), F32),
+        ((NX, 1, RX), F32),
+        ((NX, NZ, 1, RX), F32),
         ((NX, RX, FEAT), BF16),
         ((NX, RX, FEAT), BF16),
         ((NX, 1, RX), F32),
@@ -660,8 +659,8 @@
         ((NZ, RZ, FEAT), BF16),
         ((NZ, RZ, FEAT), BF16),
         ((NX, RX, FEAT), BF16),
-        ((NZ, NX, 1, RX), F32),
         ((NX, 1, RX), F32),
+        ((NX, NZ, NX, 1, RX), F32),
         ((NR, 16, 256), BF16),
         ((NR, 32, 256), BF16),
         ((NR, 32, 384), BF16),
@@ -677,7 +676,7 @@
         in_specs=[pl.BlockSpec(memory_space=pl.ANY)] * len(operands),
         out_specs=tuple(vmem(len(outs))),
         scratch_shapes=[pltpu.VMEM(*part) for part in scratch]
-        + [pair(NZ), pair(NX), pair(NX), pair(NX), pair(NZ), pair(NZ), pair(NX), pair(NZ), pair(NX)]
+        + [pair(NX * NZ), pair(NX), pair(NX), pair(NZ), pair(NZ), pair(NX), pair(NX * NZ)]
         + [pltpu.SemaphoreType.DMA((2, 4, NR)), pltpu.SemaphoreType.DMA((10,))]
         + [pltpu.SemaphoreType.DMA((2, 4, NR))],
         compiler_params=pltpu.CompilerParams(

time: 76.8 us -> 75.3 us (0.980)
  Pallas kernels: 76 us -> 74.5 us
    pallas_call x1, Pallas kernels: 74.2 us -> 72.7 us  [run_step(): pl.pallas_call(step_kernel, out_shape=tuple((jax.ShapeDtypeStruct(*out) f...]
where the time goes in v4:
time: 75.3 us; the launch traced here: 75.1 us
  Pallas kernels  74.5 us (99%)
    pallas_call x1, Pallas kernels, run_step(): pl.pallas_call(step_kernel, out_shape=tuple((jax.ShapeDtypeStruct(*out) f...  72.7 us
    pallas_call x1, Pallas kernels, adam_all(): pl.pallas_call(adam_kernel, out_shape=tuple(shapes), in_specs=vmem(9), ou...  1.79 us

profile of v4, /device:TPU:1, one launch (start us, length us, event | category | flops | bytes accessed | tf_op | source)
XLA Modules:
  0.0 75.1 jit_solution(6179641965107175154)
XLA Ops:
  0.6 72.7 %run_step.1 = (f32[16,256]{1,0:T(8,128)}, f32[32,256]{1,0:T(8,128)}, f32[32,384]{1,0:T(8,128)}, f32[1,256]{1,0:T(1,128)}, f32[4,1,128]{2,1,0:T(1,128)}) custom-call(bf16[2,512,128]{2,1,0:T(8,128)(2,1)} %codes_hbm.1, s32[1,8,512]{2,1,0:T(8,128)} %bins_hbm.1, s32[1,512]{1,0:T(1,128)} %entry_hbm.1, s32[1,512]{1,0:T(1,128)} %exit_hbm.1, s32[4,1,128]{2,1,0:T(1,128)} %bitcast.2, ...), custom_call_target="tpu_custom_call" | custom-call | tf_op jit(solution)/shard_map/run_step/pallas_call | solution.py:673
  73.3 1.8 %adam_all.1 = (f32[3,1,16,256]{3,2,1,0:T(8,128)}, f32[3,1,32,256]{3,2,1,0:T(8,128)}, f32[3,1,32,384]{3,2,1,0:T(8,128)}, f32[3,1,144]{2,1,0:T(1,128)}, f32[4,1,128]{2,1,0:T(1,128)}) custom-call(f32[3,1,16,256]{3,2,1,0:T(8,128)} %refs_0_.1, f32[3,1,32,256]{3,2,1,0:T(8,128)} %refs_1_.1, f32[3,1,32,384]{3,2,1,0:T(8,128)} %refs_2_.1, f32[3,1,144]{2,1,0:T(1,128)} %refs_3_.1, ...), custom_call_target="tpu_custom_call" | custom-call | tf_op jit(solution)/shard_map/adam_all/pallas_call | solution.py:706

commit v5 on v4

--- a/solution.py
+++ b/solution.py
@@ -57,14 +57,15 @@
 
 
 def z_sums(table, own_z):
-    column = jnp.zeros((NX, 1, RX), F32)
-    lower = jnp.zeros((NX, 1, RX), F32)
-    upper = jnp.zeros((NX, 1, RX), F32)
+    column = [jnp.zeros((1, RX), F32) for _ in range(NX)]
+    lower, upper = list(column), list(column)
     for z in range(NZ):
-        rows = table[:, z]
-        column = column + rows
-        lower = lower + rows * (z < own_z).astype(F32)
-        upper = upper + rows * (z > own_z).astype(F32)
+        under, over = (z < own_z).astype(F32), (z > own_z).astype(F32)
+        for x in range(NX):
+            rows = table[x * NZ + z]
+            column[x] = column[x] + rows
+            lower[x] = lower[x] + rows * under
+            upper[x] = upper[x] + rows * over
     return column, lower, upper
 
 
@@ -231,72 +232,56 @@
             barrier, inc=1, device_id={"rays": lax.rem(me + step, NR)}, device_id_type=MESH
         )
 
-    def move_x(step, source, target, sems):
-        x = along_x(step)
-        return remote(
-            source(x), target.at[own_x], sems.at[0, step], sems.at[1, step], at(x, own_z)
-        )
+    def arrived(sent, got, count, sems, peer):
+        first = pl.ds(0, count)
+        remote(sent.at[first], got.at[first], sems.at[0], sems.at[1], peer).wait()
 
     def spread_x(source, target, sems):
         for step in (2, 1, 3):
-            move_x(step, source, target, sems).start()
-
-    def wait_x(source, target, sems, steps=(1, 3, 2)):
-        for step in steps:
-            x = along_x(NX - step)
-            remote(source(x), target.at[x], sems.at[0, step], sems.at[1, step], at(x, own_z)).wait()
+            x = along_x(step)
+            remote(source(x), target.at[own_x], sems.at[0], sems.at[1], at(x, own_z)).start()
+
+    def wait_x(sent, got, sems):
+        arrived(sent, got, NX - 1, sems, at(along_x(1), own_z))
 
     def spread_z(source, target, sems):
         for step in far_first(NZ):
             z = along_z(step)
-            remote(
-                source(z), target.at[own_z], sems.at[0, step], sems.at[1, step], at(own_x, z)
-            ).start()
-
-    def wait_z(source, target, sems):
-        for step in far_first(NZ)[::-1]:
-            z = along_z(NZ - step)
-            remote(source(z), target.at[z], sems.at[0, step], sems.at[1, step], at(own_x, z)).wait()
+            remote(source(z), target.at[own_z], sems.at[0], sems.at[1], at(own_x, z)).start()
+
+    def wait_z(sent, got, sems):
+        arrived(sent, got, NZ - 1, sems, at(own_x, along_z(1)))
 
     def spread_all(source, target, sems):
         for far_x, far_z in far_regions():
             x, z = along_x(far_x), along_z(far_z)
-            index = far_x * NZ + far_z
-            remote(
-                source(x), target.at[own_x, own_z], sems.at[0, index], sems.at[1, index], at(x, z)
-            ).start()
-
-    def wait_all(source, target, sems):
-        for far_x, far_z in far_regions()[::-1]:
-            x, z = along_x(NX - far_x), along_z(NZ - far_z)
-            index = far_x * NZ + far_z
-            remote(
-                source(x), target.at[x, z], sems.at[0, index], sems.at[1, index], at(x, z)
-            ).wait()
+            remote(source(x), target.at[place], sems.at[0], sems.at[1], at(x, z)).start()
+
+    def wait_all(table, sems):
+        arrived(table, table, NX * NZ - 1, sems, at(along_x(1), own_z))
 
     def spread_rays(kind, source, target):
         for step in range(1, NR):
             peer = lax.rem(me + step, NR)
             remote(
                 source.at[peer],
-                target.at[step],
-                sem_rays.at[0, kind, step],
-                sem_rays.at[1, kind, step],
+                target.at[me],
+                sem_rays.at[0, kind],
+                sem_rays.at[1, kind],
                 {"rays": peer},
             ).start()
+        target[me] = jnp.zeros(target.shape[1:], target.dtype)
 
     def gather_rays(kind, source, target, total):
-        for step in range(1, NR):
-            origin = lax.rem(me + NR - step, NR)
-            remote(
-                source.at[origin],
-                target.at[step],
-                sem_rays.at[0, kind, step],
-                sem_rays.at[1, kind, step],
-                {"rays": origin},
-            ).wait()
-            total = total + target[step].astype(F32)
-        return total
+        first = pl.ds(0, NR - 1)
+        remote(
+            source.at[first],
+            target.at[first],
+            sem_rays.at[0, kind],
+            sem_rays.at[1, kind],
+            {"rays": lax.rem(me + 1, NR)},
+        ).wait()
+        return total + jnp.sum(target[...].astype(F32), 0)
 
     loads = [
         pltpu.make_async_copy(source, target, sem_load.at[index])
@@ -333,21 +318,21 @@
             remote(
                 weights[kind](me),
                 weights[kind](me),
-                sem_weight.at[0, kind, step],
-                sem_weight.at[1, kind, step],
+                sem_weight.at[0, kind],
+                sem_weight.at[1, kind],
                 {"rays": lax.rem(me + step, NR)},
             ).start()
 
     def wait_weights(kind):
-        for step in range(1, NR):
-            origin = lax.rem(me + NR - step, NR)
-            remote(
-                weights[kind](origin),
-                weights[kind](origin),
-                sem_weight.at[0, kind, step],
-                sem_weight.at[1, kind, step],
-                {"rays": origin},
-            ).wait()
+        array, count = ((w_in, 16), (w_mid, 32), (vec_ref, 1), (w_feat, 32))[kind]
+        first = array.at[pl.ds(0, count * (NR - 1))]
+        remote(
+            first,
+            first,
+            sem_weight.at[0, kind],
+            sem_weight.at[1, kind],
+            {"rays": lax.rem(me + 1, NR)},
+        ).wait()
 
     unit = depth_scale / (NX * NZ * BINS)
     lane = lax.broadcasted_iota(jnp.int32, (RX, RX), 1)
@@ -429,7 +414,7 @@
     before, total = sum_before(optical)
     depth_send[...] = total
     spread_all(lambda x: depth_send.at[x], depth_all, sem_depth)
-    depth_all[own_x, own_z] = depth_send[own_x]
+    depth_all[place] = depth_send[own_x]
     optical_rows[...] = optical
     before_rows[...] = before
     weight_rows[...] = jnp.exp(-before) * one_less_exp(optical)
@@ -449,13 +434,19 @@
 
         @pl.when(index < NX - 1)
         def _():
-            move_x(index + 1, lambda x: partial_send.at[x], partial_x, sem_partial).start()
+            remote(
+                partial_send.at[x],
+                partial_x.at[own_x],
+                sem_partial.at[0],
+                sem_partial.at[1],
+                at(x, own_z),
+            ).start()
 
         return carry
 
     lax.fori_loop(0, NX, colour_part, 0)
     partial_x[own_x] = partial_send[own_x]
-    wait_all(lambda x: depth_send.at[x], depth_all, sem_depth)
+    wait_all(depth_all, sem_depth)
     below, above = x_sums(*z_sums(depth_all, own_z))
     onward = onward_ref[own_x] == 0
     trans = [jnp.exp(-jnp.where(onward, below[x], above[x])) for x in range(NX)]
@@ -464,7 +455,7 @@
     trans_all[own_x] = trans_send[own_x]
     spread_x(lambda x: trans_send.at[x], trans_all, sem_trans)
     columns = jnp.transpose(jnp.concatenate(trans + trans, 0))
-    wait_x(lambda x: partial_send.at[x], partial_x, sem_partial)
+    wait_x(partial_send, partial_x, sem_partial)
     total = jnp.zeros((RX, FEAT), F32)
     for x in range(NX):
         total = total + columns[:, x : x + 1] * partial_x[x].astype(F32)
@@ -482,11 +473,11 @@
     wanted = target_ref[pl.ds(start, 2 * RZ), :].astype(F32)
     odd = lax.rem(own_z, 2).astype(F32)
     wanted = wanted[:RZ] * (1.0 - odd) + wanted[RZ:] * odd
-    wait_z(lambda z: pieces.at[z], pieces_z, sem_piece)
+    wait_z(pieces, pieces_z, sem_piece)
     rendered = jnp.sum(pieces_z[...].astype(F32), 0)
     grad_z[own_z] = (rendered - wanted).astype(BF16)
     spread_z(lambda z: grad_z.at[own_z], grad_z, sem_grad_z)
-    wait_x(lambda x: trans_send.at[x], trans_all, sem_trans)
+    wait_x(trans_send, trans_all, sem_trans)
 
     def coef_part(x, carry):
         columns = jnp.transpose(trans_all[x] * weight_rows[x])
@@ -497,10 +488,17 @@
         return carry
 
     lax.fori_loop(0, NX, coef_part, 0)
-    wait_z(lambda z: grad_z.at[own_z], grad_z, sem_grad_z)
+    wait_z(grad_z, grad_z, sem_grad_z)
     grad_float = grad_z[...].astype(F32).reshape(RX, FEAT)
     grad_all[own_x] = grad_float.astype(BF16)
-    spread_x(lambda x: grad_all.at[own_x], grad_all, sem_grad)
+    for step in (2, 1, 3):
+        remote(
+            grad_all.at[own_x],
+            grad_all.at[own_x],
+            sem_grad.at[0, step],
+            sem_grad.at[1, step],
+            at(along_x(step), own_z),
+        ).start()
     grid = jnp.zeros((RX, RX), F32)
     for x in range(NX):
         dots = jnp.sum(grad_float * partial_x[x].astype(F32), -1, keepdims=True)
@@ -509,14 +507,21 @@
     for x in range(NX):
         region_send[x] = grid[x : x + 1] * trans_send[x]
     spread_all(lambda x: region_send, region_all, sem_region)
-    region_all[own_x, own_z] = region_send[...]
+    region_all[place] = region_send[...]
 
     def feat_part(index, carry):
         x = along_x(index)
 
         @pl.when(index > 0)
         def _():
-            wait_x(lambda x: grad_all.at[own_x], grad_all, sem_grad, (NX - index,))
+            step = NX - index
+            remote(
+                grad_all.at[own_x],
+                grad_all.at[x],
+                sem_grad.at[0, step],
+                sem_grad.at[1, step],
+                at(x, own_z),
+            ).wait()
 
         grads = grad_all[x].astype(F32)
         grid = jnp.zeros((RX, RX), F32)
@@ -539,14 +544,19 @@
         jnp.exp(-(before_rows[...] + optical_rows[...])) * samples - later
     )
     dense_scale = span_rows[...] * jax.nn.sigmoid(raw_rows[...])
-    wait_all(lambda x: region_send, region_all, sem_region)
-    above = jnp.zeros((NX, 1, RX), F32)
-    below = jnp.zeros((NX, 1, RX), F32)
+    wait_all(region_all, sem_region)
+    above = [jnp.zeros((1, RX), F32) for _ in range(NX)]
+    below = list(above)
     for x in range(NX):
         for z in range(NZ):
-            rows = region_all[:, z, x]
-            above = above + rows * (x * NZ + z > place).astype(F32)
-            below = below + rows * (x * NZ + z < place).astype(F32)
+            over = (x * NZ + z > place).astype(F32)
+            under = (x * NZ + z < place).astype(F32)
+            for quarter in range(NX):
+                rows = region_all[quarter * NZ + z, x]
+                above[quarter] = above[quarter] + rows * over
+                below[quarter] = below[quarter] + rows * under
+    above = jnp.stack(above)
+    below = jnp.stack(below)
     after = jnp.where(onward_ref[...] == 0, above, below)
     after_out[...] = after
     dense_grad = ((local_grad - after) * dense_scale).astype(BF16).astype(F32)
@@ -604,8 +614,8 @@
 
 
 def run_step(*operands):
-    def pair(count):
-        return pltpu.SemaphoreType.DMA((2, count))
+    def pair(*count):
+        return pltpu.SemaphoreType.DMA((2, *count))
 
     outs = (((16, 256), F32), ((32, 256), F32), ((32, 384), F32), ((1, WIDE), F32))
     outs += (((NX, 1, RX), F32),)
@@ -650,7 +660,7 @@
         ((8, HID), F32),
         ((NX, RX, SLOTS), F32),
         ((NX, 1, RX), F32),
-        ((NX, NZ, 1, RX), F32),
+        ((NX * NZ, 1, RX), F32),
         ((NX, RX, FEAT), BF16),
         ((NX, RX, FEAT), BF16),
         ((NX, 1, RX), F32),
@@ -660,7 +670,7 @@
         ((NZ, RZ, FEAT), BF16),
         ((NX, RX, FEAT), BF16),
         ((NX, 1, RX), F32),
-        ((NX, NZ, NX, 1, RX), F32),
+        ((NX * NZ, NX, 1, RX), F32),
         ((NR, 16, 256), BF16),
         ((NR, 32, 256), BF16),
         ((NR, 32, 384), BF16),
@@ -676,9 +686,8 @@
         in_specs=[pl.BlockSpec(memory_space=pl.ANY)] * len(operands),
         out_specs=tuple(vmem(len(outs))),
         scratch_shapes=[pltpu.VMEM(*part) for part in scratch]
-        + [pair(NX * NZ), pair(NX), pair(NX), pair(NZ), pair(NZ), pair(NX), pair(NX * NZ)]
-        + [pltpu.SemaphoreType.DMA((2, 4, NR)), pltpu.SemaphoreType.DMA((10,))]
-        + [pltpu.SemaphoreType.DMA((2, 4, NR))],
+        + [pair(), pair(), pair(), pair(), pair(), pair(NX), pair()]
+        + [pair(4), pltpu.SemaphoreType.DMA((10,)), pair(4)],
         compiler_params=pltpu.CompilerParams(
             collective_id=0, has_side_effects=True, vmem_limit_bytes=60 * 2**20
         ),

time: 75.3 us -> 71.1 us (0.944)
  Pallas kernels: 74.5 us -> 70.3 us
    pallas_call x1, Pallas kernels: 72.7 us -> 68.5 us  [run_step(): pl.pallas_call(step_kernel, out_shape=tuple((jax.ShapeDtypeStruct(*out) f...]
where the time goes in v5:
time: 71.1 us; the launch traced here: 70.9 us
  Pallas kernels  70.3 us (99%)
    pallas_call x1, Pallas kernels, run_step(): pl.pallas_call(step_kernel, out_shape=tuple((jax.ShapeDtypeStruct(*out) f...  68.5 us
    pallas_call x1, Pallas kernels, adam_all(): pl.pallas_call(adam_kernel, out_shape=tuple(shapes), in_specs=vmem(9), ou...  1.79 us

profile of v5, /device:TPU:1, one launch (start us, length us, event | category | flops | bytes accessed | tf_op | source)
XLA Modules:
  0.0 70.9 jit_solution(13255948461773718052)
XLA Ops:
  0.6 68.5 %run_step.1 = (f32[16,256]{1,0:T(8,128)}, f32[32,256]{1,0:T(8,128)}, f32[32,384]{1,0:T(8,128)}, f32[1,256]{1,0:T(1,128)}, f32[4,1,128]{2,1,0:T(1,128)}) custom-call(bf16[2,512,128]{2,1,0:T(8,128)(2,1)} %codes_hbm.1, s32[1,8,512]{2,1,0:T(8,128)} %bins_hbm.1, s32[1,512]{1,0:T(1,128)} %entry_hbm.1, s32[1,512]{1,0:T(1,128)} %exit_hbm.1, s32[4,1,128]{2,1,0:T(1,128)} %bitcast.2, ...), custom_call_target="tpu_custom_call" | custom-call | tf_op jit(solution)/shard_map/run_step/pallas_call | solution.py:683
  69.1 1.8 %adam_all.1 = (f32[3,1,16,256]{3,2,1,0:T(8,128)}, f32[3,1,32,256]{3,2,1,0:T(8,128)}, f32[3,1,32,384]{3,2,1,0:T(8,128)}, f32[3,1,144]{2,1,0:T(1,128)}, f32[4,1,128]{2,1,0:T(1,128)}) custom-call(f32[3,1,16,256]{3,2,1,0:T(8,128)} %refs_0_.1, f32[3,1,32,256]{3,2,1,0:T(8,128)} %refs_1_.1, f32[3,1,32,384]{3,2,1,0:T(8,128)} %refs_2_.1, f32[3,1,144]{2,1,0:T(1,128)} %refs_3_.1, ...), custom_call_target="tpu_custom_call" | custom-call | tf_op jit(solution)/shard_map/adam_all/pallas_call | solution.py:715

commit v6 on v5

--- a/solution.py
+++ b/solution.py
@@ -208,6 +208,8 @@
     sem_rays,
     sem_load,
     sem_weight,
+    column_sem,
+    line_sem,
 ):
     place = lax.axis_index("region")
     me = lax.axis_index("rays")
@@ -223,9 +225,13 @@
         return {"region": x * NZ + z}
 
     barrier = pltpu.get_barrier_semaphore()
-    for far_x, far_z in far_regions():
+    for step in (1, NZ - 1):
         pl.semaphore_signal(
-            barrier, inc=1, device_id=at(along_x(far_x), along_z(far_z)), device_id_type=MESH
+            barrier, inc=1, device_id=at(own_x, along_z(step)), device_id_type=MESH
+        )
+    for step in (2, 1, 3):
+        pl.semaphore_signal(
+            barrier, inc=1, device_id=at(along_x(step), own_z), device_id_type=MESH
         )
     for step in range(1, NR):
         pl.semaphore_signal(
@@ -255,7 +261,7 @@
     def spread_all(source, target, sems):
         for far_x, far_z in far_regions():
             x, z = along_x(far_x), along_z(far_z)
-            remote(source(x), target.at[place], sems.at[0], sems.at[1], at(x, z)).start()
+            remote(source(x, z), target.at[place], sems.at[0], sems.at[1], at(x, z)).start()
 
     def wait_all(table, sems):
         arrived(table, table, NX * NZ - 1, sems, at(along_x(1), own_z))
@@ -344,6 +350,23 @@
     weights[3](me)[...] = feat_own[...].astype(BF16)
     vec_ref[me] = jnp.zeros((1, WIDE), F32)
     vec_ref[me, :, pl.ds(0, PART)] = vec_own[...].astype(BF16).astype(F32)
+    pl.semaphore_wait(barrier, NX + NR)
+    for kind in range(4):
+        spread_weights(kind)
+
+    def tell_line(reach):
+        for step in (reach, NZ - reach):
+            pl.semaphore_signal(
+                line_sem.at[reach.bit_length() - 1],
+                inc=1,
+                device_id=at(own_x, along_z(step)),
+                device_id_type=MESH,
+            )
+
+    def hear_line(reach):
+        pl.semaphore_wait(line_sem.at[reach.bit_length() - 1], 2)
+
+    tell_line(1)
     for load in loads[4:]:
         load.wait()
     for total in (g_in, g_mid, g_feat, sum_dense):
@@ -353,6 +376,9 @@
         enc_t[x, pl.ds(IN, 16), :] = ones
         h1_t[x, pl.ds(HID, 16), :] = ones
         h2_t[x, pl.ds(HID, 16), :] = ones
+
+    hear_line(1)
+    tell_line(2)
 
     def code_part(x, carry):
         lanes = pl.ds(pl.multiple_of(x * RX, RX), RX)
@@ -370,15 +396,19 @@
         return carry
 
     lax.fori_loop(0, NX, code_part, 0)
-    pl.semaphore_wait(barrier, NX * NZ + NR - 2)
-    for kind in range(4):
-        spread_weights(kind)
+    hear_line(2)
+    tell_line(4)
 
     def turn_code(x, carry):
         enc_t[x, pl.ds(0, IN), :] = jnp.transpose(enc[x])
         return carry
 
     lax.fori_loop(0, NX, turn_code, 0)
+    hear_line(4)
+    for step in (2, 1, 3):
+        pl.semaphore_signal(
+            column_sem, inc=1, device_id=at(along_x(step), own_z), device_id_type=MESH
+        )
     for kind in range(3):
         wait_weights(kind)
     row = jnp.zeros((1, 1280), F32)
@@ -413,7 +443,8 @@
     optical = soft * span_rows[...]
     before, total = sum_before(optical)
     depth_send[...] = total
-    spread_all(lambda x: depth_send.at[x], depth_all, sem_depth)
+    pl.semaphore_wait(column_sem, NX - 1)
+    spread_all(lambda x, z: depth_send.at[x], depth_all, sem_depth)
     depth_all[place] = depth_send[own_x]
     optical_rows[...] = optical
     before_rows[...] = before
@@ -504,10 +535,25 @@
         dots = jnp.sum(grad_float * partial_x[x].astype(F32), -1, keepdims=True)
         grid = jnp.where(lane == x, dots, grid)
     grid = jnp.transpose(grid)
+    grads = [grid[x : x + 1] * trans_send[x] for x in range(NX)]
     for x in range(NX):
-        region_send[x] = grid[x : x + 1] * trans_send[x]
-    spread_all(lambda x: region_send, region_all, sem_region)
-    region_all[place] = region_send[...]
+        over, under = jnp.zeros((1, RX), F32), jnp.zeros((1, RX), F32)
+        for other in range(NX):
+            if other > x:
+                over = over + grads[other]
+            if other < x:
+                under = under + grads[other]
+        level = jnp.where(onward, over, under)
+        region_send[3 * x] = level
+        region_send[3 * x + 1] = level + jnp.where(onward, grads[x], 0.0)
+        region_send[3 * x + 2] = level + jnp.where(onward, 0.0, grads[x])
+
+    def after_row(x, z):
+        side = (own_z > z).astype(jnp.int32) + 2 * (own_z < z).astype(jnp.int32)
+        return region_send.at[3 * x + side]
+
+    spread_all(after_row, region_all, sem_region)
+    region_all[place] = region_send[3 * own_x]
 
     def feat_part(index, carry):
         x = along_x(index)
@@ -545,19 +591,7 @@
     )
     dense_scale = span_rows[...] * jax.nn.sigmoid(raw_rows[...])
     wait_all(region_all, sem_region)
-    above = [jnp.zeros((1, RX), F32) for _ in range(NX)]
-    below = list(above)
-    for x in range(NX):
-        for z in range(NZ):
-            over = (x * NZ + z > place).astype(F32)
-            under = (x * NZ + z < place).astype(F32)
-            for quarter in range(NX):
-                rows = region_all[quarter * NZ + z, x]
-                above[quarter] = above[quarter] + rows * over
-                below[quarter] = below[quarter] + rows * under
-    above = jnp.stack(above)
-    below = jnp.stack(below)
-    after = jnp.where(onward_ref[...] == 0, above, below)
+    after = jnp.sum(region_all[...].reshape(NX, NZ, 1, RX), 1)
     after_out[...] = after
     dense_grad = ((local_grad - after) * dense_scale).astype(BF16).astype(F32)
     for x in range(NX):
@@ -669,8 +703,8 @@
         ((NZ, RZ, FEAT), BF16),
         ((NZ, RZ, FEAT), BF16),
         ((NX, RX, FEAT), BF16),
-        ((NX, 1, RX), F32),
-        ((NX * NZ, NX, 1, RX), F32),
+        ((3 * NX, 1, RX), F32),
+        ((NX * NZ, 1, RX), F32),
         ((NR, 16, 256), BF16),
         ((NR, 32, 256), BF16),
         ((NR, 32, 384), BF16),
@@ -687,7 +721,8 @@
         out_specs=tuple(vmem(len(outs))),
         scratch_shapes=[pltpu.VMEM(*part) for part in scratch]
         + [pair(), pair(), pair(), pair(), pair(), pair(NX), pair()]
-        + [pair(4), pltpu.SemaphoreType.DMA((10,)), pair(4)],
+        + [pair(4), pltpu.SemaphoreType.DMA((10,)), pair(4), pltpu.SemaphoreType.REGULAR]
+        + [pltpu.SemaphoreType.REGULAR((3,))],
         compiler_params=pltpu.CompilerParams(
             collective_id=0, has_side_effects=True, vmem_limit_bytes=60 * 2**20
         ),

time: 71.1 us -> 67.2 us (0.945)
  Pallas kernels: 70.3 us -> 66.3 us
    pallas_call x1, Pallas kernels: 68.5 us -> 64.5 us  [run_step(): pl.pallas_call(step_kernel, out_shape=tuple((jax.ShapeDtypeStruct(*out) f...]
where the time goes in v6:
time: 67.2 us; the launch traced here: 67 us
  Pallas kernels  66.3 us (99%)
    pallas_call x1, Pallas kernels, run_step(): pl.pallas_call(step_kernel, out_shape=tuple((jax.ShapeDtypeStruct(*out) f...  64.5 us
    pallas_call x1, Pallas kernels, adam_all(): pl.pallas_call(adam_kernel, out_shape=tuple(shapes), in_specs=vmem(9), ou...  1.79 us

profile of v6, /device:TPU:1, one launch (start us, length us, event | category | flops | bytes accessed | tf_op | source)
XLA Modules:
  0.0 67.0 jit_solution(9882026455686388548)
XLA Ops:
  0.6 64.5 %run_step.1 = (f32[16,256]{1,0:T(8,128)}, f32[32,256]{1,0:T(8,128)}, f32[32,384]{1,0:T(8,128)}, f32[1,256]{1,0:T(1,128)}, f32[4,1,128]{2,1,0:T(1,128)}) custom-call(bf16[2,512,128]{2,1,0:T(8,128)(2,1)} %codes_hbm.1, s32[1,8,512]{2,1,0:T(8,128)} %bins_hbm.1, s32[1,512]{1,0:T(1,128)} %entry_hbm.1, s32[1,512]{1,0:T(1,128)} %exit_hbm.1, s32[4,1,128]{2,1,0:T(1,128)} %bitcast.2, ...), custom_call_target="tpu_custom_call" | custom-call | tf_op jit(solution)/shard_map/run_step/pallas_call | solution.py:717
  65.2 1.8 %adam_all.1 = (f32[3,1,16,256]{3,2,1,0:T(8,128)}, f32[3,1,32,256]{3,2,1,0:T(8,128)}, f32[3,1,32,384]{3,2,1,0:T(8,128)}, f32[3,1,144]{2,1,0:T(1,128)}, f32[4,1,128]{2,1,0:T(1,128)}) custom-call(f32[3,1,16,256]{3,2,1,0:T(8,128)} %refs_0_.1, f32[3,1,32,256]{3,2,1,0:T(8,128)} %refs_1_.1, f32[3,1,32,384]{3,2,1,0:T(8,128)} %refs_2_.1, f32[3,1,144]{2,1,0:T(1,128)} %refs_3_.1, ...), custom_call_target="tpu_custom_call" | custom-call | tf_op jit(solution)/shard_map/adam_all/pallas_call | solution.py:750

commit v7 on v6

--- a/solution.py
+++ b/solution.py
@@ -117,10 +117,6 @@
 
 def to_row_groups(values):
     return jnp.sum(values.reshape(values.shape[0] // 8, 8, values.shape[1]), 0)
-
-
-def dot_nt(left, right):
-    return lax.dot_general(left, right, (((1,), (1,)), ((), ())), preferred_element_type=F32)
 
 
 def step_kernel(
@@ -153,6 +149,8 @@
     w_mid,
     w_feat,
     vec_ref,
+    w_mid_t,
+    w_feat_t,
     enc,
     h1,
     h2,
@@ -404,11 +402,6 @@
         return carry
 
     lax.fori_loop(0, NX, turn_code, 0)
-    hear_line(4)
-    for step in (2, 1, 3):
-        pl.semaphore_signal(
-            column_sem, inc=1, device_id=at(along_x(step), own_z), device_id_type=MESH
-        )
     for kind in range(3):
         wait_weights(kind)
     row = jnp.zeros((1, 1280), F32)
@@ -437,7 +430,13 @@
         raw_rows[x] = jnp.transpose(grid)[:SLOTS]
         return carry
 
-    lax.fori_loop(0, NX, hidden_part, 0)
+    lax.fori_loop(0, 2, hidden_part, 0)
+    hear_line(4)
+    for step in (2, 1, 3):
+        pl.semaphore_signal(
+            column_sem, inc=1, device_id=at(along_x(step), own_z), device_id_type=MESH
+        )
+    lax.fori_loop(2, NX, hidden_part, 0)
     raw = raw_rows[...]
     soft = jnp.maximum(raw, 0.0) + jnp.log1p(jnp.exp(-jnp.abs(raw)))
     optical = soft * span_rows[...]
@@ -500,6 +499,8 @@
         return carry
 
     lax.fori_loop(0, NX, turn_part, 0)
+    w_mid_t[...] = jnp.transpose(w_mid[...])
+    w_feat_t[...] = jnp.transpose(w_feat[...])
     start = pl.multiple_of(own_x * RX + (own_z // 2) * (2 * RZ), 2 * RZ)
     wanted = target_ref[pl.ds(start, 2 * RZ), :].astype(F32)
     odd = lax.rem(own_z, 2).astype(F32)
@@ -522,7 +523,7 @@
     wait_z(grad_z, grad_z, sem_grad_z)
     grad_float = grad_z[...].astype(F32).reshape(RX, FEAT)
     grad_all[own_x] = grad_float.astype(BF16)
-    for step in (2, 1, 3):
+    for step in (1, 3, 2):
         remote(
             grad_all.at[own_x],
             grad_all.at[own_x],
@@ -556,11 +557,13 @@
     region_all[place] = region_send[3 * own_x]
 
     def feat_part(index, carry):
-        x = along_x(index)
+        late = (index == 2).astype(jnp.int32) - (index == 3).astype(jnp.int32)
+        offset = index + late
+        x = along_x(offset)
 
         @pl.when(index > 0)
         def _():
-            step = NX - index
+            step = NX - offset
             remote(
                 grad_all.at[own_x],
                 grad_all.at[x],
@@ -578,7 +581,7 @@
             cgrad[rows, :] = (coef[x, rows, :] * grads).astype(BF16)
         sample_rows[x] = jnp.transpose(grid)[:SLOTS]
         g_feat[...] += jnp.dot(h2_t[x], cgrad[...], preferred_element_type=F32)
-        hgrad[x] = dot_nt(cgrad[...], w_feat[...])
+        hgrad[x] = jnp.dot(cgrad[...], w_feat_t[...], preferred_element_type=F32)
         return carry
 
     lax.fori_loop(0, NX, feat_part, 0)
@@ -618,7 +621,9 @@
 
     def in_part(x, carry):
         first[...] = jnp.where(
-            h1[x].astype(F32) > 0.0, dot_nt(second[x], w_mid[...]), 0.0
+            h1[x].astype(F32) > 0.0,
+            jnp.dot(second[x], w_mid_t[...], preferred_element_type=F32),
+            0.0,
         ).astype(BF16)
         g_in[...] += jnp.dot(enc_t[x], first[...], preferred_element_type=F32)
         return carry
@@ -668,6 +673,8 @@
         ((HID, HID), BF16),
         ((HID, FEAT), BF16),
         ((NR, 1, WIDE), F32),
+        ((HID, HID), BF16),
+        ((FEAT, HID), BF16),
         ((NX, ROWS, IN), BF16),
         ((NX, ROWS, HID), BF16),
         ((NX, ROWS, HID), BF16),

time: 67.2 us -> 67.9 us (1.010)
  Pallas kernels: 66.3 us -> 67.1 us
    pallas_call x1, Pallas kernels: 64.5 us -> 65.3 us  [run_step(): pl.pallas_call(step_kernel, out_shape=tuple((jax.ShapeDtypeStruct(*out) f...]
where the time goes in v7:
time: 67.9 us; the launch traced here: 67.7 us
  Pallas kernels  67.1 us (99%)
    pallas_call x1, Pallas kernels, run_step(): pl.pallas_call(step_kernel, out_shape=tuple((jax.ShapeDtypeStruct(*out) f...  65.3 us
    pallas_call x1, Pallas kernels, adam_all(): pl.pallas_call(adam_kernel, out_shape=tuple(shapes), in_specs=vmem(9), ou...  1.79 us

profile of v7, /device:TPU:1, one launch (start us, length us, event | category | flops | bytes accessed | tf_op | source)
XLA Modules:
  0.0 67.7 jit_solution(2740987587778514102)
XLA Ops:
  0.6 65.3 %run_step.1 = (f32[16,256]{1,0:T(8,128)}, f32[32,256]{1,0:T(8,128)}, f32[32,384]{1,0:T(8,128)}, f32[1,256]{1,0:T(1,128)}, f32[4,1,128]{2,1,0:T(1,128)}) custom-call(bf16[2,512,128]{2,1,0:T(8,128)(2,1)} %codes_hbm.1, s32[1,8,512]{2,1,0:T(8,128)} %bins_hbm.1, s32[1,512]{1,0:T(1,128)} %entry_hbm.1, s32[1,512]{1,0:T(1,128)} %exit_hbm.1, s32[4,1,128]{2,1,0:T(1,128)} %bitcast.2, ...), custom_call_target="tpu_custom_call" | custom-call | tf_op jit(solution)/shard_map/run_step/pallas_call | solution.py:724
  65.9 1.8 %adam_all.1 = (f32[3,1,16,256]{3,2,1,0:T(8,128)}, f32[3,1,32,256]{3,2,1,0:T(8,128)}, f32[3,1,32,384]{3,2,1,0:T(8,128)}, f32[3,1,144]{2,1,0:T(1,128)}, f32[4,1,128]{2,1,0:T(1,128)}) custom-call(f32[3,1,16,256]{3,2,1,0:T(8,128)} %refs_0_.1, f32[3,1,32,256]{3,2,1,0:T(8,128)} %refs_1_.1, f32[3,1,32,384]{3,2,1,0:T(8,128)} %refs_2_.1, f32[3,1,144]{2,1,0:T(1,128)} %refs_3_.1, ...), custom_call_target="tpu_custom_call" | custom-call | tf_op jit(solution)/shard_map/adam_all/pallas_call | solution.py:757

commit v8 on v7

--- a/solution.py
+++ b/solution.py
@@ -523,7 +523,7 @@
     wait_z(grad_z, grad_z, sem_grad_z)
     grad_float = grad_z[...].astype(F32).reshape(RX, FEAT)
     grad_all[own_x] = grad_float.astype(BF16)
-    for step in (1, 3, 2):
+    for step in (2, 1, 3):
         remote(
             grad_all.at[own_x],
             grad_all.at[own_x],

time: 67.9 us -> 67.9 us (level)
  no operation moved by 1% of the time
where the time goes in v8:
time: 67.9 us; the launch traced here: 67.7 us
  Pallas kernels  67.1 us (99%)
    pallas_call x1, Pallas kernels, run_step(): pl.pallas_call(step_kernel, out_shape=tuple((jax.ShapeDtypeStruct(*out) f...  65.3 us
    pallas_call x1, Pallas kernels, adam_all(): pl.pallas_call(adam_kernel, out_shape=tuple(shapes), in_specs=vmem(9), ou...  1.79 us

profile of v8, /device:TPU:1, one launch (start us, length us, event | category | flops | bytes accessed | tf_op | source)
XLA Modules:
  0.0 67.7 jit_solution(7699284932919033580)
XLA Ops:
  0.6 65.3 %run_step.1 = (f32[16,256]{1,0:T(8,128)}, f32[32,256]{1,0:T(8,128)}, f32[32,384]{1,0:T(8,128)}, f32[1,256]{1,0:T(1,128)}, f32[4,1,128]{2,1,0:T(1,128)}) custom-call(bf16[2,512,128]{2,1,0:T(8,128)(2,1)} %codes_hbm.1, s32[1,8,512]{2,1,0:T(8,128)} %bins_hbm.1, s32[1,512]{1,0:T(1,128)} %entry_hbm.1, s32[1,512]{1,0:T(1,128)} %exit_hbm.1, s32[4,1,128]{2,1,0:T(1,128)} %bitcast.2, ...), custom_call_target="tpu_custom_call" | custom-call | tf_op jit(solution)/shard_map/run_step/pallas_call | solution.py:724
  65.9 1.8 %adam_all.1 = (f32[3,1,16,256]{3,2,1,0:T(8,128)}, f32[3,1,32,256]{3,2,1,0:T(8,128)}, f32[3,1,32,384]{3,2,1,0:T(8,128)}, f32[3,1,144]{2,1,0:T(1,128)}, f32[4,1,128]{2,1,0:T(1,128)}) custom-call(f32[3,1,16,256]{3,2,1,0:T(8,128)} %refs_0_.1, f32[3,1,32,256]{3,2,1,0:T(8,128)} %refs_1_.1, f32[3,1,32,384]{3,2,1,0:T(8,128)} %refs_2_.1, f32[3,1,144]{2,1,0:T(1,128)} %refs_3_.1, ...), custom_call_target="tpu_custom_call" | custom-call | tf_op jit(solution)/shard_map/adam_all/pallas_call | solution.py:757
